TPU v7x, 32 devices: a whole 2x2x4 slice. The times are simulated.
32 devices in a mesh: facet: 8 (over y, x, core), pix: 4 (over z).
Axes of the slice: x: 2, y: 2, z: 4, core: 2. Of those that a mesh axis runs over, the one named last changes fastest.
Arguments:
- image: float32 [32, 512, 512], P(('facet', 'pix')), may hold values from 0 to 1
- visibilities: float32 [2, 32, 256, 128], P(None, ('facet', 'pix')), may hold values from -6 to 6
- tile_index: int32 [32, 256], P(('facet', 'pix')), may hold values from 0 to 1023
- cells: int32 [32, 256, 128], P(('facet', 'pix')), may hold values from 0 to 1023
- block_count: int32 [32], P(('facet', 'pix')), may hold values from 64 to 256, as said below
- lowrank_dual: float32 [32, 512, 512], P(None, ('facet', 'pix')), may hold values from -6 to 6
- wavelet_dual: float32 [32, 512, 512], P(None, ('facet', 'pix')), may hold values from -4 to 4
- wavelet_bound: float32 [32], replicated, may hold values from 0.2 to 2
Outputs:
- image_next: float32 [32, 512, 512], P(('facet', 'pix'))
- lowrank_next: float32 [32, 512, 512], P(None, ('facet', 'pix'))
- wavelet_next: float32 [32, 512, 512], P(None, ('facet', 'pix'))
Inputs may be any that keep to these rules, and one draw needn't show every extreme that they name: `cells`: cell within the tile is its row times 128 plus its column. `block_count`: blocks at or after a channel's count are padding; some channel has all 256 blocks live.
All inputs are finite; a program needn't handle non-finite values.
Results may differ from a plain program's by a relative error of at most 0.0003.
Values sent between devices are 32-bit elements; how exact they have to be, the bound alone decides.
No kernel may reach another device: no remote copies, remote signals or barrier semaphores. Data moves between devices by JAX's collectives and lax.ppermute only.
A program may use at most 128 MiB of HBM per device.

v0:
```python
import functools
import math

import jax
import jax.numpy as jnp
import numpy as np
from jax import lax
from jax.experimental import pallas as pl
from jax.experimental.pallas import tpu as pltpu
from jax.sharding import PartitionSpec as P

TILE_R = 8
TILE_C = 128
NS_STEPS = 5
GROUP = 16
RING = ("facet", "pix")

highest = lax.Precision.HIGHEST
tau_step = 0.5
sigma_step = 1.0
f32 = jnp.float32
bf16 = jnp.bfloat16
VMEM_BYTES = 56 * 1024 * 1024


def gauss(n):
    d = np.arange(n)[:, None] - np.arange(n)[None, :]
    return np.exp(-0.5 * d.astype(np.float64) ** 2)


def small_tables(height, width):
    rows, cols = 2 * height, 2 * width
    m = np.arange(height)
    n = np.arange(width)
    near = gauss(TILE_R) @ np.exp(-2j * np.pi * np.arange(TILE_R)[:, None] * m[None, :] / rows)
    period = rows // TILE_R
    turn = np.exp(
        -2j * np.pi * (np.arange(period)[:, None] * np.arange(period)[None, :] % period) / period
    )
    span = np.exp(-2j * np.pi * n[:, None] * np.arange(TILE_C)[None, :] / cols) @ gauss(TILE_C)
    span = span / height
    bands = cols // TILE_C
    swing = np.exp(-2j * np.pi * np.arange(bands)[:, None] * np.arange(8)[None, :] / bands)
    swing = np.broadcast_to(swing[:, :, None], (bands, 8, TILE_C))
    assert bands == 8 and period == 128
    out = []
    for table in (near, turn, span, swing):
        out += [np.ascontiguousarray(table.real, np.float32), np.ascontiguousarray(table.imag, np.float32)]
    return out


def split(x):
    high = x.astype(bf16)
    return high, (x - high.astype(f32)).astype(bf16)


def dot3(a_hi, a_lo, b_hi, b_lo):
    return (
        jnp.dot(a_hi, b_hi, preferred_element_type=f32)
        + jnp.dot(a_lo, b_hi, preferred_element_type=f32)
        + jnp.dot(a_hi, b_lo, preferred_element_type=f32)
    )


def nt(a, b):
    return lax.dot_general(a, b, (((1,), (1,)), ((), ())), preferred_element_type=f32)


def plan_blocks(tiles, count, bands, chunks):
    blocks = tiles.shape[0]
    index = jnp.arange(blocks, dtype=jnp.int32)
    band = jnp.where(index < count, tiles % bands, bands)
    same = band[:, None] == band[None, :]
    rank = jnp.sum((same & (index[None, :] < index[:, None])).astype(jnp.int32), axis=1)
    sizes = jnp.sum((band[None, :] == jnp.arange(bands, dtype=jnp.int32)[:, None]).astype(jnp.int32), axis=1)
    groups = (sizes + GROUP - 1) // GROUP
    upto = jnp.arange(bands)[None, :] <= jnp.arange(bands)[:, None]
    ends = jnp.sum(jnp.where(upto, groups[None, :], 0), axis=1)
    first = ends - groups
    mine = band[:, None] == jnp.arange(bands, dtype=jnp.int32)[None, :]
    slot = jnp.sum(jnp.where(mine, first[None, :] * GROUP, 0), axis=1) + rank
    slot = jnp.where(band < bands, slot, -1)
    spots = jnp.arange(chunks * GROUP, dtype=jnp.int32)
    code = index * 128 + tiles // bands
    spare = blocks * 128
    entries = spare + jnp.sum(jnp.where(slot[None, :] == spots[:, None], code[None, :] - spare, 0), axis=1)
    which = jnp.sum((jnp.arange(chunks)[:, None] >= ends[None, :]).astype(jnp.int32), axis=1)
    which = jnp.minimum(which, bands - 1)
    tail = jnp.stack([ends[-1], count])
    return entries.astype(jnp.int32), jnp.concatenate([which, tail]).astype(jnp.int32)


def misfit_kernel(
    entries, bands_of, image, cells, vis,
    near_re, near_im, turn_re, turn_im, span_re, span_im, swing_re, swing_im,
    wt_hi, wt_lo, wc_hi, wc_lo, rt_hi, rt_lo,
    y_hi, y_lo, hist, wg_hi, wg_lo, o_ref, r_ref,
):
    chunks = rt_hi.shape[0]
    bands = wc_hi.shape[0]
    side = image.shape[0]
    blocks = cells.shape[0]
    tall = wt_hi.shape[0]

    def build_rows(a, carry):
        pr = jnp.broadcast_to(turn_re[pl.ds(a, 1), :], (8, 128))
        pi = jnp.broadcast_to(turn_im[pl.ds(a, 1), :], (8, 128))
        for t in range(side // 128):
            at = slice(t * 128, (t + 1) * 128)
            nr, ni = near_re[:, at], near_im[:, at]
            both = jnp.concatenate([pr * nr - pi * ni, pr * ni + pi * nr], axis=0)
            high, low = split(both)
            wt_hi[a, :, at] = high
            wt_lo[a, :, at] = low
        return carry

    lax.fori_loop(0, tall, build_rows, 0, unroll=4)

    x_hi, x_lo = split(image[...])

    def build_cols(b, carry):
        cr = swing_re[b][None]
        ci = swing_im[b][None]
        sr = span_re[...].reshape(side // 8, 8, 128)
        si = span_im[...].reshape(side // 8, 8, 128)
        re = (cr * sr - ci * si).reshape(side, 128)
        im = (cr * si + ci * sr).reshape(side, 128)
        high, low = split(jnp.concatenate([re, im], axis=1))
        wc_hi[b] = high
        wc_lo[b] = low
        high, low = split(dot3(x_hi, x_lo, high, low))
        y_hi[b] = high
        y_lo[b] = low
        return carry

    lax.fori_loop(0, bands, build_cols, 0)

    hist[blocks] = jnp.zeros((24, 128), f32)
    rows8 = lax.broadcasted_iota(jnp.int32, (8, 128), 0)
    rows128 = lax.broadcasted_iota(jnp.int32, (128, 128), 0)

    def count_cells(g, carry):
        base = pl.multiple_of(g * GROUP, GROUP)
        q = cells[pl.ds(base, GROUP), :]
        qr = q // TILE_C
        qc = q - qr * TILE_C
        parts = []
        for p in range(2):
            v = vis[p, pl.ds(base, GROUP), :]
            high = v.astype(bf16).astype(f32)
            parts += [high, v - high]
        for s in range(GROUP):
            row = (rows8 == qr[s : s + 1]).astype(f32)
            pieces = [row] + [row * part[s : s + 1] for part in parts]
            lhs = jnp.concatenate(pieces + [jnp.zeros((8, 128), f32)], axis=0).astype(bf16)
            hot = (rows128 == qc[s : s + 1]).astype(f32).astype(bf16)
            out = nt(lhs, hot)
            hist[base + s, 0:8] = out[0:8]
            hist[base + s, 8:16] = out[8:16] + out[16:24]
            hist[base + s, 16:24] = out[24:32] + out[32:40]
        return carry

    lax.fori_loop(0, (bands_of[chunks + 1] + GROUP - 1) // GROUP, count_cells, 0)

    def work(c, carry):
        b = bands_of[c]
        for s in range(GROUP):
            a = entries[c * GROUP + s] & 127
            wg_hi[16 * s : 16 * s + 16] = wt_hi[a]
            wg_lo[16 * s : 16 * s + 16] = wt_lo[a]
        o_ref[...] = dot3(wg_hi[...], wg_lo[...], y_hi[b], y_lo[b])
        for s in range(GROUP):
            k = entries[c * GROUP + s] // 128
            top = slice(16 * s, 16 * s + 8)
            low = slice(16 * s + 8, 16 * s + 16)
            model_re = o_ref[top, 0:128] - o_ref[low, 128:256]
            model_im = o_ref[top, 128:256] + o_ref[low, 0:128]
            many = hist[k, 0:8]
            g_re = many * model_re - hist[k, 8:16]
            g_im = many * model_im - hist[k, 16:24]
            r_ref[top, 0:128] = g_re
            r_ref[top, 128:256] = g_im
            r_ref[low, 0:128] = g_im
            r_ref[low, 128:256] = -g_re
        high, low = split(r_ref[...].T)
        rt_hi[c] = high
        rt_lo[c] = low
        return carry

    lax.fori_loop(0, bands_of[chunks], work, 0)


def adjoint_kernel(entries, bands_of, rt_hi, rt_lo, wt_hi, wt_lo, wc_hi, wc_lo, out, z, wg_hi, wg_lo, acc):
    chunks = rt_hi.shape[0]
    bands = wc_hi.shape[0]
    z[...] = jnp.zeros_like(z)

    def gather(c, carry):
        b = bands_of[c]
        for s in range(GROUP):
            a = entries[c * GROUP + s] & 127
            wg_hi[16 * s : 16 * s + 16] = wt_hi[a]
            wg_lo[16 * s : 16 * s + 16] = wt_lo[a]
        z[b] += dot3(rt_hi[c], rt_lo[c], wg_hi[...], wg_lo[...])
        return carry

    lax.fori_loop(0, bands_of[chunks], gather, 0)
    acc[...] = jnp.zeros_like(acc)

    def back(b, carry):
        high, low = split(z[b])
        acc[...] += dot3(wc_hi[b], wc_lo[b], high, low)
        return carry

    lax.fori_loop(0, bands, back, 0)
    out[...] = acc[...].T


def whole(n):
    return [pl.BlockSpec(memory_space=pltpu.VMEM) for _ in range(n)]


def misfit_groups(plane, vis, cells, entries, bands_of):
    side = plane.shape[0]
    tables = [jnp.asarray(t) for t in small_tables(*plane.shape)]
    chunks = entries.shape[0] // GROUP
    bands = 2 * side // TILE_C
    tall = 2 * side // TILE_R
    blocks = cells.shape[0]
    shapes = [(tall, 16, side)] * 2 + [(bands, side, 256)] * 2 + [(chunks, 256, 256)] * 2
    return pl.pallas_call(
        misfit_kernel,
        out_shape=[jax.ShapeDtypeStruct(s, bf16) for s in shapes],
        grid_spec=pltpu.PrefetchScalarGridSpec(
            num_scalar_prefetch=2,
            grid=(),
            in_specs=whole(3 + len(tables)),
            out_specs=whole(6),
            scratch_shapes=[
                pltpu.VMEM((bands, side, 256), bf16),
                pltpu.VMEM((bands, side, 256), bf16),
                pltpu.VMEM((blocks + 1, 24, 128), f32),
                pltpu.VMEM((256, side), bf16),
                pltpu.VMEM((256, side), bf16),
                pltpu.VMEM((256, 256), f32),
                pltpu.VMEM((256, 256), f32),
            ],
        ),
        compiler_params=pltpu.CompilerParams(vmem_limit_bytes=VMEM_BYTES),
        name="misfit",
    )(entries, bands_of, plane, cells, vis, *tables)


def adjoint_image(entries, bands_of, rt_hi, rt_lo, wt_hi, wt_lo, wc_hi, wc_lo):
    bands, side, _ = wc_hi.shape
    return pl.pallas_call(
        adjoint_kernel,
        out_shape=jax.ShapeDtypeStruct((side, side), f32),
        grid_spec=pltpu.PrefetchScalarGridSpec(
            num_scalar_prefetch=2,
            grid=(),
            in_specs=whole(6),
            out_specs=whole(1)[0],
            scratch_shapes=[
                pltpu.VMEM((bands, 256, side), f32),
                pltpu.VMEM((256, side), bf16),
                pltpu.VMEM((256, side), bf16),
                pltpu.VMEM((side, side), f32),
            ],
        ),
        compiler_params=pltpu.CompilerParams(vmem_limit_bytes=VMEM_BYTES),
        name="adjoint",
    )(entries, bands_of, rt_hi, rt_lo, wt_hi, wt_lo, wc_hi, wc_lo)


def gram_kernel(dual, image, out):
    total = dual.shape[0]
    channels = out.shape[0]
    rows = total // channels
    high, low = split(dual[...] + sigma_step * image[...])
    full = nt(high, high) + nt(high, low) + nt(low, high)
    i = lax.broadcasted_iota(jnp.int32, (total, total), 0)
    j = lax.broadcasted_iota(jnp.int32, (total, total), 1)
    full = jnp.where(i % rows == j % rows, full, 0.0)
    ci = lax.broadcasted_iota(jnp.int32, (channels, total), 0)
    cj = lax.broadcasted_iota(jnp.int32, (channels, total), 1)
    pick = (cj // rows == ci).astype(f32).astype(bf16)

    def gather_left(x):
        a, rest = split(x)
        b, c = split(x - a.astype(f32))
        return sum(jnp.dot(pick, part, preferred_element_type=f32) for part in (a, b, c))

    half = gather_left(full)
    a, b = split(half)
    c = (half - a.astype(f32) - b.astype(f32)).astype(bf16)
    out[...] = nt(a, pick) + nt(b, pick) + nt(c, pick)


def lowrank_kernel(ridge, gram, dual, image, detail, lowrank, direction):
    total = dual.shape[0]
    channels = gram.shape[-1]
    rows = total // channels
    g = gram[0]
    for p in range(1, gram.shape[0]):
        g = g + gram[p]
    ci = lax.broadcasted_iota(jnp.int32, (channels, channels), 0)
    cj = lax.broadcasted_iota(jnp.int32, (channels, channels), 1)
    identity = (ci == cj).astype(f32)
    shifted = g + ridge * identity
    trace = jnp.sum(shifted * identity, keepdims=True)
    current = shifted / trace
    inverse = identity
    for turn in range(NS_STEPS):
        factor = 1.5 * identity - 0.5 * jnp.dot(inverse, current, precision=highest)
        current = jnp.dot(current, factor, precision=highest)
        inverse = jnp.dot(factor, inverse, precision=highest)
    root = inverse * (math.sqrt(ridge) * lax.rsqrt(trace))
    i = lax.broadcasted_iota(jnp.int32, (total, total), 0)
    j = lax.broadcasted_iota(jnp.int32, (total, total), 1)
    si = lax.broadcasted_iota(jnp.int32, (total, channels), 0)
    sj = lax.broadcasted_iota(jnp.int32, (total, channels), 1)
    pick = (si // rows == sj).astype(f32).astype(bf16)
    match = i % rows == j % rows

    def spread(x):
        wide = jnp.dot(pick, x, preferred_element_type=f32).astype(bf16)
        return jnp.where(match, nt(wide, pick), 0.0).astype(bf16)

    root_hi, root_lo = split(root)
    high, low = split(dual[...] + sigma_step * image[...])
    result = dot3(spread(root_hi), spread(root_lo), high, low)
    lowrank[...] = result
    direction[...] = 2.0 * result - dual[...] + detail[...]


def local_gram(dual, image, channels):
    return pl.pallas_call(
        gram_kernel,
        out_shape=jax.ShapeDtypeStruct((channels, channels), f32),
        in_specs=whole(2),
        out_specs=whole(1)[0],
        compiler_params=pltpu.CompilerParams(vmem_limit_bytes=VMEM_BYTES),
        name="gram",
    )(dual, image)


def lowrank_update(gram, dual, image, detail, ridge):
    return pl.pallas_call(
        functools.partial(lowrank_kernel, ridge),
        out_shape=[jax.ShapeDtypeStruct(dual.shape, f32)] * 2,
        in_specs=whole(4),
        out_specs=whole(2),
        compiler_params=pltpu.CompilerParams(vmem_limit_bytes=VMEM_BYTES),
        name="lowrank",
    )(gram, dual, image, detail)


def row_difference(rimmed):
    return rimmed[:, 1:-1] - 0.5 * (rimmed[:, :-2] + rimmed[:, 2:])


def column_difference(field):
    padded = jnp.pad(field, ((0, 0), (0, 0), (1, 1)))
    return padded[:, :, 1:-1] - 0.5 * (padded[:, :, :-2] + padded[:, :, 2:])


def neighbours(shard, width):
    devices = lax.axis_size(RING)
    up = [(i, i + 1) for i in range(devices - 1)]
    down = [(j, i) for i, j in up]
    return lax.ppermute(shard[:, -width:], RING, up), lax.ppermute(shard[:, :width], RING, down)


def per_device(
    image, visibilities, tile_index, cells, block_count, lowrank_dual, wavelet_dual, wavelet_bound
):
    side = image.shape[-1]
    channels, rows_here, _ = lowrank_dual.shape
    devices = lax.axis_size(RING)
    pieces = lax.axis_size("pix")
    here = lax.axis_index(RING)
    flat = (channels * rows_here, side)

    facet_image = lax.all_to_all(
        image.reshape(devices, rows_here, side), RING, split_axis=0, concat_axis=0, tiled=True
    )
    dual_before, dual_after = neighbours(wavelet_dual, 1)

    bands = 2 * side // TILE_C
    chunks = tile_index.shape[1] // GROUP + bands
    entries, bands_of = plan_blocks(tile_index[0], block_count[0], bands, chunks)
    groups = misfit_groups(image[0], visibilities[:, 0], cells[0], entries, bands_of)
    wt_hi, wt_lo, wc_hi, wc_lo, rt_hi, rt_lo = groups
    facet_image, rt_hi = lax.optimization_barrier((facet_image, rt_hi))

    image_before, image_after = neighbours(facet_image, 2)
    gram = local_gram(lowrank_dual.reshape(flat), facet_image.reshape(flat), channels)
    grams = [gram] + [
        lax.ppermute(gram, "pix", [(i, (i + s) % pieces) for i in range(pieces)]) for s in range(1, pieces)
    ]

    bound = wavelet_bound[:, None, None]
    rimmed = jnp.concatenate([image_before, facet_image, image_after], axis=1)
    dual_rimmed = jnp.concatenate([dual_before, wavelet_dual, dual_after], axis=1)
    next_rimmed = jnp.clip(
        dual_rimmed + sigma_step * column_difference(row_difference(rimmed)), -bound, bound
    )
    wavelet_next = next_rimmed[:, 1:-1]
    row = lax.broadcasted_iota(jnp.int32, (1, rows_here + 2, 1), 1) + here * rows_here
    inside = (row >= 1) & (row <= side)
    pushed = jnp.where(inside, 2.0 * next_rimmed - dual_rimmed, 0.0)
    back_detail = column_difference(row_difference(pushed))

    ridge = float(rows_here * side * pieces)
    lowrank_next, direction = lowrank_update(
        jnp.stack(grams),
        lowrank_dual.reshape(flat),
        facet_image.reshape(flat),
        back_detail.reshape(flat),
        ridge,
    )
    direction, rt_hi = lax.optimization_barrier((direction, rt_hi))
    returned = lax.all_to_all(
        direction.reshape(channels, rows_here, side), RING, split_axis=0, concat_axis=0, tiled=True
    )
    gradient = adjoint_image(entries, bands_of, rt_hi, rt_lo, wt_hi, wt_lo, wc_hi, wc_lo)
    returned = returned.reshape(side, side)
    image_next = jnp.maximum(image[0] - tau_step * (gradient + returned), 0.0)
    return (image_next[None], lowrank_next.reshape(lowrank_dual.shape), wavelet_next)


def solution(mesh):
    return jax.shard_map(
        per_device,
        mesh=mesh,
        in_specs=(
            P(RING, None, None),
            P(None, RING, None, None),
            P(RING, None),
            P(RING, None, None),
            P(RING),
            P(None, RING, None),
            P(None, RING, None),
            P(),
        ),
        out_specs=(P(RING, None, None), P(None, RING, None), P(None, RING, None)),
        check_vma=False,
    )
```

profile of v0, /device:TPU:1, one launch (start us, length us, event | category | flops | bytes accessed | tf_op | source)
XLA Modules:
  0.0 117.1 jit_solution(3932591945316189428)
XLA Ops:
  0.6 0.0 copy-start.3
  0.6 7.1 %all-to-all-start = ((f32[32,16,512]{2,1,0:T(8,128)}), f32[32,16,512]{2,1,0:T(8,128)S(1)}, u32[]{:S(2)}, u32[]{:S(2)}) async-start(f32[32,16,512]{2,1,0:T(8,128)} %bitcast.33), calls=%async_computation | async-start | bytes 2097152 | tf_op jit(solution)/shard_map/all_to_all | solution.py:385
  8.4 0.0 copy-done.3
  8.4 0.1 convert_reduce_fusion.1
  8.6 0.1 select_reduce_fusion.2
  8.7 0.6 slice.48
  9.3 0.1 select_reduce_fusion.1
  9.4 0.2 convert_reduce_fusion
  9.6 0.1 convert_reduce_fusion.2
  9.7 1.3 %pad_add_fusion.bands_of = s32[26]{0:T(128)} fusion(s32[1]{0:T(128)} %copy.19, s32[1]{0:T(128)} %slice.48, s32[24]{0:T(128)S(1)} %broadcast_minimum_fusion), kind=kLoop, calls=%fused_computation.60 | loop fusion | flops 52 | bytes 208 | tf_op jit(solution)/shard_map/concatenate | solution.py:90
  11.0 0.1 select_reduce_fusion
  11.1 0.6 broadcast_add_fusion.entries
  11.7 26.0 %misfit.1 = (bf16[128,16,512]{2,1,0:T(8,128)(2,1)}, bf16[128,16,512]{2,1,0:T(8,128)(2,1)}, bf16[8,512,256]{2,1,0:T(8,128)(2,1)}, bf16[8,512,256]{2,1,0:T(8,128)(...) custom-call(s32[384]{0:T(512)} %broadcast_add_fusion.entries, s32[26]{0:T(128)} %pad_add_fusion.bands_of, ...), custom_call_target="tpu_custom_call" | custom-call | tf_op jit(solution)/shard_map/misfit/pallas_call | solution.py:231
  37.7 1.3 %fusion.20 = (f32[32,1,512]{2,1,0:T(1,128)S(1)}, f32[32,1,512]{2,1,0:T(1,128)S(1)}) fusion(f32[32,16,512]{2,1,0:T(8,128)} %param.22), kind=kLoop, calls=%fused_computation.64 | loop fusion | bytes 262144 | tf_op jit(solution)/shard_map/slice | solution.py:372
  39.1 0.0 all-to-all-done
  39.1 0.0 copy-start
  39.1 0.1 fusion.19
  39.2 0.8 copy-done
  40.1 3.8 %gram.1 = f32[32,32]{1,0:T(8,128)} custom-call(f32[512,512]{1,0:T(8,128)} %bitcast.35, f32[512,512]{1,0:T(8,128)} %bitcast.31), custom_call_target="tpu_custom_call" | custom-call | tf_op jit(solution)/shard_map/gram/pallas_call | solution.py:338
  43.8 0.0 copy-start.2
  43.8 5.2 %collective-permute-start = (f32[32,32]{1,0:T(8,128)}, f32[32,32]{1,0:T(8,128)S(1)}, u32[]{:S(2)}, u32[]{:S(2)}) collective-permute-start(f32[32,32]{1,0:T(8,128)} %gram.1), channel_id=1, source_target_pairs={{0,1},{1,2},{2,3},{3,0},{4,5},{5,6},{6,7},{7,4},{8,9},{9,10},{10,1... | collective-permute-start | bytes 12296 | tf_op jit(solution)/shard_map/ppermute | solution.py:400
  49.0 0.0 collective-permute-start.1
  49.0 2.1 %collective-permute-start.2 = (f32[32,32]{1,0:T(8,128)}, f32[32,32]{1,0:T(8,128)S(1)}, u32[]{:S(2)}, u32[]{:S(2)}) collective-permute-start(f32[32,32]{1,0:T(8,128)} %gram.1), channel_id=1, source_target_pairs={{0,3},{1,0},{2,1},{3,2},{4,7},{5,4},{6,5},{7,6},{8,11},{9,8},{10,9... | collective-permute-start | bytes 12296 | tf_op jit(solution)/shard_map/ppermute | solution.py:400
  51.1 1.9 %collective-permute-start.5 = (f32[32,2,512]{2,1,0:T(2,128)S(1)}, f32[32,2,512]{2,1,0:T(2,128)S(1)}, u32[]{:S(2)}, u32[]{:S(2)}) collective-permute-start(f32[32,2,512]{2,1,0:T(2,128)S(1)} %get-tuple-element.29), channel_id=1, source_target_pairs={{0,1},{1,2},{2,3},{3,4},{4,5},{5,6},{6,7},{7,8},{8,9},{9,10},{10,1... | collective-permute-start | bytes 393224 | tf_op jit(solution)/shard_map/ppermute | solution.py:372
  53.0 5.4 %collective-permute-start.6 = (f32[32,2,512]{2,1,0:T(2,128)S(1)}, f32[32,2,512]{2,1,0:T(2,128)S(1)}, u32[]{:S(2)}, u32[]{:S(2)}) collective-permute-start(f32[32,2,512]{2,1,0:T(2,128)S(1)} %get-tuple-element.30), channel_id=1, source_target_pairs={{1,0},{2,1},{3,2},{4,3},{5,4},{6,5},{7,6},{8,7},{9,8},{10,9},{11,1... | collective-permute-start | bytes 393224 | tf_op jit(solution)/shard_map/ppermute | solution.py:372
  58.5 0.0 copy-done.4
  58.5 0.0 collective-permute-done
  58.5 1.9 %collective-permute-start.3 = (f32[32,1,512]{2,1,0:T(1,128)S(1)}, f32[32,1,512]{2,1,0:T(1,128)S(1)}, u32[]{:S(2)}, u32[]{:S(2)}) collective-permute-start(f32[32,1,512]{2,1,0:T(1,128)S(1)} %get-tuple-element.31), channel_id=1, source_target_pairs={{0,1},{1,2},{2,3},{3,4},{4,5},{5,6},{6,7},{7,8},{8,9},{9,10},{10,1... | collective-permute-start | bytes 196616 | tf_op jit(solution)/shard_map/ppermute | solution.py:372
  60.4 0.0 collective-permute-done.1
  60.4 5.4 %collective-permute-start.4 = (f32[32,1,512]{2,1,0:T(1,128)S(1)}, f32[32,1,512]{2,1,0:T(1,128)S(1)}, u32[]{:S(2)}, u32[]{:S(2)}) collective-permute-start(f32[32,1,512]{2,1,0:T(1,128)S(1)} %get-tuple-element.32), channel_id=1, source_target_pairs={{1,0},{2,1},{3,2},{4,3},{5,4},{6,5},{7,6},{8,7},{9,8},{10,9},{11,1... | collective-permute-start | bytes 196616 | tf_op jit(solution)/shard_map/ppermute | solution.py:372
  65.9 0.0 collective-permute-done.2
  65.9 1.3 %pad_maximum_fusion.3.gram = f32[4,32,32]{2,1,0:T(8,128)} fusion(f32[1,32,32]{2,1,0:T(8,128)S(1)} %bitcast.45, f32[1,32,32]{2,1,0:T(8,128)S(1)} %bitcast.44, f32[1,32,32]{2,1,0:T(8,128)S(1)} %bitcast.43, f32[1,32,32]{2,1,0:T(8,128)} %bitcast.42), kind=kLoop, calls=%fused_computation.32 | loop fusion | flops 12288 | bytes 32768 | tf_op jit(solution)/shard_map/stack | solution.py:417
  67.2 0.0 collective-permute-done.5
  67.2 0.0 collective-permute-done.6
  67.3 2.6 %fusion.6 = f32[32,18,512]{2,1,0:T(8,128)S(1)} fusion(f32[32,2,512]{2,1,0:T(2,128)S(1)} %collective-permute-done.6, f32[32,16,512]{2,1,0:T(8,128)} %copy-done, f32[32,2,512]{2,1,0:T(2,128)S(1)} %collective-permute-done.5), kind=kLoop, calls=%fused_computation.9 | loop fusion | flops 2064384 | bytes 2490368 | tf_op jit(solution)/shard_map/sub | solution.py:360
  69.8 0.0 collective-permute-done.3
  69.9 0.0 collective-permute-done.4
  69.9 0.0 copy-done.2
  69.9 1.1 subtract_select_fusion
  71.0 0.2 fusion.12
  71.2 1.6 %fusion.10 = f32[32,16,512]{2,1,0:T(8,128)} fusion(f32[32,16,512]{2,1,0:T(8,128)S(1)} %fusion.12), kind=kLoop, calls=%fused_computation.19 | loop fusion | flops 786432 | bytes 2097152 | tf_op jit(solution)/shard_map/sub | solution.py:365
  72.8 6.5 %lowrank.1 = (f32[512,512]{1,0:T(8,128)}, f32[512,512]{1,0:T(8,128)}) custom-call(f32[4,32,32]{2,1,0:T(8,128)} %pad_maximum_fusion.3.gram, f32[512,512]{1,0:T(8,128)} %bitcast.36, f32[512,512]{1,0:T(8,128)} %bitcast.32, f32[512,512]{1,0:T(8,128)} %bitcast.37), custom_call_target="tpu_custom_call" | custom-call | tf_op jit(solution)/shard_map/lowrank/pallas_call | solution.py:349
  79.3 8.5 %all-to-all-start.1 = ((f32[32,16,512]{2,1,0:T(8,128)}), f32[32,16,512]{2,1,0:T(8,128)}, u32[]{:S(2)}, u32[]{:S(2)}) async-start(f32[32,16,512]{2,1,0:T(8,128)} %bitcast.38), calls=%async_computation.1 | async-start | bytes 2097152 | tf_op jit(solution)/shard_map/all_to_all | solution.py:424
  87.8 1.2 slice.65
  88.9 17.9 %adjoint.1 = f32[512,512]{1,0:T(8,128)} custom-call(s32[384]{0:T(512)} %broadcast_add_fusion.entries, s32[26]{0:T(128)} %pad_add_fusion.bands_of, bf16[24,256,256]{2,1,0:T(8,128)(2,1)} %get-tuple-element.19.rt_hi, bf16[24,256,256]{2,1,0:T(8,128)(2,1)} %get-tuple-element.20.rt_lo, bf16[128,16,512]{2,1,0:T(8,128)(2,1)} %get-tuple-element.21.wt_hi, ...), custom_call_target="tpu_custom_call" | custom-call | tf_op jit(solution)/shard_map/adjoint/pallas_call | solution.py:256
  106.8 7.4 %all-to-all-done.1 = f32[32,16,512]{2,1,0:T(8,128)} async-done(((f32[32,16,512]{2,1,0:T(8,128)}), f32[32,16,512]{2,1,0:T(8,128)}, u32[]{:S(2)}, u32[]{:S(2)}) %all-to-all-start.1) | async-done | bytes 1048608 | tf_op jit(solution)/shard_map/all_to_all | solution.py:424
  114.2 0.0 copy-done.1
  114.2 2.9 %fusion.15 = f32[512,512]{1,0:T(8,128)} fusion(f32[512,512]{1,0:T(8,128)} %adjoint.1, f32[32,16,512]{2,1,0:T(8,128)} %all-to-all-done.1, f32[1,512,512]{2,1,0:T(8,128)S(1)} %copy-done.1), kind=kLoop, calls=%fused_computation.26 | loop fusion | flops 1048576 | bytes 4194304 | tf_op jit(solution)/shard_map/max | solution.py:429
  (11 shorter events, 0.1 us)
Async XLA Ops:
  0.6 7.8 %copy-start.3 = (s32[1,256]{1,0:T(1,128)S(1)}, s32[1,256]{1,0:T(1,128)}, u32[]{:S(2)}) copy-start(s32[1,256]{1,0:T(1,128)} %param.18) | copy-start | bytes 3076
  0.6 38.4 %all-to-all-start = ((f32[32,16,512]{2,1,0:T(8,128)}), f32[32,16,512]{2,1,0:T(8,128)S(1)}, u32[]{:S(2)}, u32[]{:S(2)}) async-start(f32[32,16,512]{2,1,0:T(8,128)} %bitcast.33), calls=%async_computation | async-start | bytes 2097152 | tf_op jit(solution)/shard_map/all_to_all | solution.py:385
  37.7 20.7 %copy-start.4 = (f32[32]{0:T(128)S(1)}, f32[32]{0:T(128)}, u32[]{:S(2)}) copy-start(f32[32]{0:T(128)} %param.23) | copy-start | bytes 388
  39.1 1.0 copy-start
  43.8 26.0 %copy-start.2 = (f32[32,16,512]{2,1,0:T(8,128)S(1)}, f32[32,16,512]{2,1,0:T(8,128)}, u32[]{:S(2)}) copy-start(f32[32,16,512]{2,1,0:T(8,128)} %param.22) | copy-start | bytes 3145732
  43.8 14.7 %collective-permute-start = (f32[32,32]{1,0:T(8,128)}, f32[32,32]{1,0:T(8,128)S(1)}, u32[]{:S(2)}, u32[]{:S(2)}) collective-permute-start(f32[32,32]{1,0:T(8,128)} %gram.1), channel_id=1, source_target_pairs={{0,1},{1,2},{2,3},{3,0},{4,5},{5,6},{6,7},{7,4},{8,9},{9,10},{10,1... | collective-permute-start | bytes 12296 | tf_op jit(solution)/shard_map/ppermute | solution.py:400
  49.0 11.4 %collective-permute-start.1 = (f32[32,32]{1,0:T(8,128)}, f32[32,32]{1,0:T(8,128)S(1)}, u32[]{:S(2)}, u32[]{:S(2)}) collective-permute-start(f32[32,32]{1,0:T(8,128)} %gram.1), channel_id=1, source_target_pairs={{0,2},{1,3},{2,0},{3,1},{4,6},{5,7},{6,4},{7,5},{8,10},{9,11},{10,... | collective-permute-start | bytes 12296 | tf_op jit(solution)/shard_map/ppermute | solution.py:400
  49.0 16.9 %collective-permute-start.2 = (f32[32,32]{1,0:T(8,128)}, f32[32,32]{1,0:T(8,128)S(1)}, u32[]{:S(2)}, u32[]{:S(2)}) collective-permute-start(f32[32,32]{1,0:T(8,128)} %gram.1), channel_id=1, source_target_pairs={{0,3},{1,0},{2,1},{3,2},{4,7},{5,4},{6,5},{7,6},{8,11},{9,8},{10,9... | collective-permute-start | bytes 12296 | tf_op jit(solution)/shard_map/ppermute | solution.py:400
  51.1 16.2 %collective-permute-start.5 = (f32[32,2,512]{2,1,0:T(2,128)S(1)}, f32[32,2,512]{2,1,0:T(2,128)S(1)}, u32[]{:S(2)}, u32[]{:S(2)}) collective-permute-start(f32[32,2,512]{2,1,0:T(2,128)S(1)} %get-tuple-element.29), channel_id=1, source_target_pairs={{0,1},{1,2},{2,3},{3,4},{4,5},{5,6},{6,7},{7,8},{8,9},{9,10},{10,1... | collective-permute-start | bytes 393224 | tf_op jit(solution)/shard_map/ppermute | solution.py:372
  53.0 14.2 %collective-permute-start.6 = (f32[32,2,512]{2,1,0:T(2,128)S(1)}, f32[32,2,512]{2,1,0:T(2,128)S(1)}, u32[]{:S(2)}, u32[]{:S(2)}) collective-permute-start(f32[32,2,512]{2,1,0:T(2,128)S(1)} %get-tuple-element.30), channel_id=1, source_target_pairs={{1,0},{2,1},{3,2},{4,3},{5,4},{6,5},{7,6},{8,7},{9,8},{10,9},{11,1... | collective-permute-start | bytes 393224 | tf_op jit(solution)/shard_map/ppermute | solution.py:372
  58.5 11.3 %collective-permute-start.3 = (f32[32,1,512]{2,1,0:T(1,128)S(1)}, f32[32,1,512]{2,1,0:T(1,128)S(1)}, u32[]{:S(2)}, u32[]{:S(2)}) collective-permute-start(f32[32,1,512]{2,1,0:T(1,128)S(1)} %get-tuple-element.31), channel_id=1, source_target_pairs={{0,1},{1,2},{2,3},{3,4},{4,5},{5,6},{6,7},{7,8},{8,9},{9,10},{10,1... | collective-permute-start | bytes 196616 | tf_op jit(solution)/shard_map/ppermute | solution.py:372
  60.4 9.4 %collective-permute-start.4 = (f32[32,1,512]{2,1,0:T(1,128)S(1)}, f32[32,1,512]{2,1,0:T(1,128)S(1)}, u32[]{:S(2)}, u32[]{:S(2)}) collective-permute-start(f32[32,1,512]{2,1,0:T(1,128)S(1)} %get-tuple-element.32), channel_id=1, source_target_pairs={{1,0},{2,1},{3,2},{4,3},{5,4},{6,5},{7,6},{8,7},{9,8},{10,9},{11,1... | collective-permute-start | bytes 196616 | tf_op jit(solution)/shard_map/ppermute | solution.py:372
  79.3 34.9 %all-to-all-start.1 = ((f32[32,16,512]{2,1,0:T(8,128)}), f32[32,16,512]{2,1,0:T(8,128)}, u32[]{:S(2)}, u32[]{:S(2)}) async-start(f32[32,16,512]{2,1,0:T(8,128)} %bitcast.38), calls=%async_computation.1 | async-start | bytes 2097152 | tf_op jit(solution)/shard_map/all_to_all | solution.py:424
  88.9 25.2 %copy-start.1 = (f32[1,512,512]{2,1,0:T(8,128)S(1)}, f32[1,512,512]{2,1,0:T(8,128)}, u32[]{:S(2)}) copy-start(f32[1,512,512]{2,1,0:T(8,128)} %param.16) | copy-start | bytes 3145732
where the time goes:
time: 117 us
  Pallas kernels  54.2 us (46%)
  starting transfers between devices  37.6 us (32%)
  other arithmetic  12.4 us (11%)
  waiting for transfers between devices  7.37 us (6%)
  local copies, waits for them, and re-layouts  4.04 us (3%)
  between operations  1.5 us (1%)
    pallas_call x1, Pallas kernels, misfit_groups(): pl.pallas_call(misfit_kernel, out_shape=[jax.ShapeDtypeStruct(s, bf16) fo...  26 us
    pallas_call x1, Pallas kernels, adjoint_image(): pl.pallas_call(adjoint_kernel, out_shape=jax.ShapeDtypeStruct((side, side...  17.9 us
    ppermute x2, starting transfers between devices, neighbours(): lax.ppermute(shard[:, :width], RING, down)  10.9 us
    all_to_all x1, starting transfers between devices, per_device(): lax.all_to_all(direction.reshape(channels, rows_here, side), RING, split_...  8.51 us
    all_to_all x1, waiting for transfers between devices, per_device(): lax.all_to_all(direction.reshape(channels, rows_here, side), RING, split_...  7.35 us
    ppermute x3, starting transfers between devices, per_device(): lax.ppermute(gram, 'pix', [(i, (i + s) % pieces) for i in range(pieces)])  7.25 us
    all_to_all x1, starting transfers between devices, per_device(): lax.all_to_all(image.reshape(devices, rows_here, side), RING, split_axis=...  7.1 us
    pallas_call x1, Pallas kernels, lowrank_update(): pl.pallas_call(functools.partial(lowrank_kernel, ridge), out_shape=[jax.S...  6.46 us
  transfers between devices with their start and end apart: 9, of which 1 were waited for; matrix products, arithmetic and copies ran while one was open for 8% of the time, Pallas kernels for 38%

commit v1 on v0

v1 whole, which is shorter than its diff:
```python
import functools
import math

import jax
import jax.numpy as jnp
import numpy as np
from jax import lax
from jax.experimental import pallas as pl
from jax.experimental.pallas import tpu as pltpu
from jax.sharding import PartitionSpec as P

TILE_R = 8
TILE_C = 128
NS_STEPS = 5
GROUP = 16
PARTS = 4
RING = ("facet", "pix")

highest = lax.Precision.HIGHEST
tau_step = 0.5
sigma_step = 1.0
f32 = jnp.float32
bf16 = jnp.bfloat16
MIB = 1024 * 1024
BIG = 58 * MIB


def gauss(n):
    d = np.arange(n)[:, None] - np.arange(n)[None, :]
    return np.exp(-0.5 * d.astype(np.float64) ** 2)


def small_tables(height, width):
    rows, cols = 2 * height, 2 * width
    m = np.arange(height)
    n = np.arange(width)
    near = gauss(TILE_R) @ np.exp(-2j * np.pi * np.arange(TILE_R)[:, None] * m[None, :] / rows)
    period = rows // TILE_R
    turn = np.exp(
        -2j * np.pi * (np.arange(period)[:, None] * np.arange(period)[None, :] % period) / period
    )
    span = np.exp(-2j * np.pi * n[:, None] * np.arange(TILE_C)[None, :] / cols) @ gauss(TILE_C)
    span = span / height
    bands = cols // TILE_C
    swing = np.exp(-2j * np.pi * np.arange(bands)[:, None] * np.arange(8)[None, :] / bands)
    swing = np.broadcast_to(swing[:, :, None], (bands, 8, TILE_C))
    assert bands == 8 and period == 128
    near = near.reshape(TILE_R, -1, 128).transpose(1, 0, 2)
    parts = []
    for table in (span, swing, turn, near):
        parts += [table.real.reshape(-1, 128), table.imag.reshape(-1, 128)]
    return np.concatenate(parts).astype(np.float32), [len(part) for part in parts]


def table_views(table, sizes):
    views, start = [], 0
    for size in sizes:
        views.append(table.at[pl.ds(start, size)])
        start += size
    return views


def split(x):
    high = x.astype(bf16)
    return high, (x - high.astype(f32)).astype(bf16)


def dot3(a_hi, a_lo, b_hi, b_lo):
    return (
        jnp.dot(a_hi, b_hi, preferred_element_type=f32)
        + jnp.dot(a_lo, b_hi, preferred_element_type=f32)
        + jnp.dot(a_hi, b_lo, preferred_element_type=f32)
    )


def nt(a, b):
    return lax.dot_general(a, b, (((1,), (1,)), ((), ())), preferred_element_type=f32)


def plan_blocks(tiles, count, bands, chunks):
    blocks = tiles.shape[0]
    index = jnp.arange(blocks, dtype=jnp.int32)
    band = jnp.where(index < count, tiles % bands, bands)
    same = band[:, None] == band[None, :]
    rank = jnp.sum((same & (index[None, :] < index[:, None])).astype(jnp.int32), axis=1)
    sizes = jnp.sum((band[None, :] == jnp.arange(bands, dtype=jnp.int32)[:, None]).astype(jnp.int32), axis=1)
    groups = (sizes + GROUP - 1) // GROUP
    upto = jnp.arange(bands)[None, :] <= jnp.arange(bands)[:, None]
    ends = jnp.sum(jnp.where(upto, groups[None, :], 0), axis=1)
    first = ends - groups
    mine = band[:, None] == jnp.arange(bands, dtype=jnp.int32)[None, :]
    slot = jnp.sum(jnp.where(mine, first[None, :] * GROUP, 0), axis=1) + rank
    slot = jnp.where(band < bands, slot, -1)
    spots = jnp.arange(chunks * GROUP, dtype=jnp.int32)
    code = index * 128 + tiles // bands
    spare = blocks * 128
    entries = spare + jnp.sum(jnp.where(slot[None, :] == spots[:, None], code[None, :] - spare, 0), axis=1)
    which = jnp.sum((jnp.arange(chunks)[:, None] >= ends[None, :]).astype(jnp.int32), axis=1)
    which = jnp.minimum(which, bands - 1)
    return entries.astype(jnp.int32), jnp.concatenate([which, ends[-1:]]).astype(jnp.int32)


def column_band(b, span_re, span_im, swing_re, swing_im):
    side = span_re.shape[0]
    at = pl.ds(pl.multiple_of(b * 8, 8), 8)
    cr = swing_re[at][None]
    ci = swing_im[at][None]
    sr = span_re[...].reshape(side // 8, 8, TILE_C)
    si = span_im[...].reshape(side // 8, 8, TILE_C)
    re = (cr * sr - ci * si).reshape(side, TILE_C)
    im = (cr * si + ci * sr).reshape(side, TILE_C)
    return split(jnp.concatenate([re, im], axis=1))


def forward_kernel(
    sizes, live, image_in, cells_in, vis_in, table_in, y_out, hist_out,
    image, cells, vis, table, y, hist, x_hi, x_lo, in_sem, y_sem, hist_sem, spare_sem,
):
    bands = y.shape[1]
    blocks = cells.shape[0]
    reads = [
        pltpu.make_async_copy(source, to, in_sem.at[i])
        for i, (source, to) in enumerate(
            ((image_in, image), (table_in.at[pl.ds(0, table.shape[0])], table), (cells_in, cells), (vis_in, vis))
        )
    ]
    for read in reads:
        read.start()
    span_re, span_im, swing_re, swing_im = table_views(table, sizes)
    reads[0].wait()
    x_hi[...], x_lo[...] = split(image[...])
    reads[1].wait()

    def y_copy(part, b):
        return pltpu.make_async_copy(y.at[part, b], y_out.at[part, b], y_sem.at[part, b])

    def hist_copy(g):
        at = pl.ds(g * GROUP, GROUP)
        return pltpu.make_async_copy(hist.at[at], hist_out.at[at], hist_sem.at[g])

    def build_cols(b, carry):
        high, low = column_band(b, span_re, span_im, swing_re, swing_im)
        high, low = split(dot3(x_hi[...], x_lo[...], high, low))
        y[0, b] = high
        y[1, b] = low
        y_copy(0, b).start()
        y_copy(1, b).start()
        return carry

    lax.fori_loop(0, bands, build_cols, 0, unroll=2)

    reads[2].wait()
    reads[3].wait()
    hist[blocks] = jnp.zeros((24, 128), f32)
    spare = pltpu.make_async_copy(hist.at[pl.ds(blocks, 1)], hist_out.at[pl.ds(blocks, 1)], spare_sem)
    spare.start()
    rows8 = lax.broadcasted_iota(jnp.int32, (8, 128), 0)
    rows128 = lax.broadcasted_iota(jnp.int32, (128, 128), 0)

    def count_cells(g, carry):
        base = pl.multiple_of(g * GROUP, GROUP)
        q = cells[pl.ds(base, GROUP), :]
        qr = q // TILE_C
        qc = q - qr * TILE_C
        parts = []
        for p in range(2):
            v = vis[p, pl.ds(base, GROUP), :]
            high = v.astype(bf16).astype(f32)
            parts += [high, v - high]
        for s in range(GROUP):
            row = (rows8 == qr[s : s + 1]).astype(f32)
            pieces = [row] + [row * part[s : s + 1] for part in parts]
            lhs = jnp.concatenate(pieces + [jnp.zeros((8, 128), f32)], axis=0).astype(bf16)
            hot = (rows128 == qc[s : s + 1]).astype(f32).astype(bf16)
            out = nt(lhs, hot)
            hist[base + s, 0:8] = out[0:8]
            hist[base + s, 8:16] = out[8:16] + out[16:24]
            hist[base + s, 16:24] = out[24:32] + out[32:40]
        hist_copy(g).start()
        return carry

    groups = (live[0] + GROUP - 1) // GROUP
    lax.fori_loop(0, groups, count_cells, 0)

    def hist_wait(g, carry):
        hist_copy(g).wait()
        return carry

    lax.fori_loop(0, groups, hist_wait, 0)
    spare.wait()
    for part in range(2):
        for b in range(bands):
            y_copy(part, b).wait()


def adjoint_kernel(
    sizes, entries, bands_of, image_in, y_in, hist_in, table_in,
    out, image, y, hist, table, sems, wt_hi, wt_lo, z, acc, r_ref, *sets,
):
    side = image.shape[0]
    bands = y.shape[1]
    chunks = entries.shape[0] // GROUP
    reads = [
        pltpu.make_async_copy(source, to, sems.at[i])
        for i, (source, to) in enumerate(((table_in, table), (y_in, y), (hist_in, hist), (image_in, image)))
    ]
    for read in reads:
        read.start()
    span_re, span_im, swing_re, swing_im, turn_re, turn_im, near_re, near_im = table_views(table, sizes)
    reads[0].wait()
    tall = wt_hi.shape[0]
    sets = (sets[:3], sets[3:])

    def build_rows(a, carry):
        pr = jnp.broadcast_to(turn_re[pl.ds(a, 1), :], (8, 128))
        pi = jnp.broadcast_to(turn_im[pl.ds(a, 1), :], (8, 128))
        for t in range(side // 128):
            at = slice(t * 128, (t + 1) * 128)
            nr, ni = near_re[8 * t : 8 * t + 8], near_im[8 * t : 8 * t + 8]
            both = jnp.concatenate([pr * nr - pi * ni, pr * ni + pi * nr], axis=0)
            high, low = split(both)
            wt_hi[a, :, at] = high
            wt_lo[a, :, at] = low
        return carry

    lax.fori_loop(0, tall, build_rows, 0, unroll=4)
    z[...] = jnp.zeros_like(z)
    for read in reads[1:]:
        read.wait()

    def evaluate(c, refs):
        wg_hi, wg_lo, o_ref = refs
        b = bands_of[c]
        for s in range(GROUP):
            a = entries[c * GROUP + s] & 127
            wg_hi[16 * s : 16 * s + 16] = wt_hi[a]
            wg_lo[16 * s : 16 * s + 16] = wt_lo[a]
        o_ref[...] = dot3(wg_hi[...], wg_lo[...], y[0, b], y[1, b])

    def spread(c, refs):
        wg_hi, wg_lo, o_ref = refs
        for s in range(GROUP):
            k = entries[c * GROUP + s] // 128
            top = slice(16 * s, 16 * s + 8)
            low = slice(16 * s + 8, 16 * s + 16)
            model_re = o_ref[top, 0:128] - o_ref[low, 128:256]
            model_im = o_ref[top, 128:256] + o_ref[low, 0:128]
            many = hist[k, 0:8]
            g_re = many * model_re - hist[k, 8:16]
            g_im = many * model_im - hist[k, 16:24]
            r_ref[top, 0:128] = g_re
            r_ref[top, 128:256] = g_im
            r_ref[low, 0:128] = g_im
            r_ref[low, 128:256] = -g_re
        rt_hi, rt_lo = split(r_ref[...].T)
        z[bands_of[c]] += dot3(rt_hi, rt_lo, wg_hi[...], wg_lo[...])

    evaluate(0, sets[0])

    def work(i, carry):
        evaluate(2 * i + 1, sets[1])
        spread(2 * i, sets[0])
        evaluate(2 * i + 2, sets[0])
        spread(2 * i + 1, sets[1])
        return carry

    lax.fori_loop(0, (bands_of[chunks] + 1) // 2, work, 0)
    acc[...] = jnp.zeros_like(acc)

    def back(b, carry):
        wc_hi, wc_lo = column_band(b, span_re, span_im, swing_re, swing_im)
        high, low = split(z[b])
        acc[...] += dot3(wc_hi, wc_lo, high, low)
        return carry

    lax.fori_loop(0, bands, back, 0, unroll=2)
    out[...] = image[...] - tau_step * acc[...].T


def whole(n):
    return [pl.BlockSpec(memory_space=pltpu.VMEM) for _ in range(n)]


def in_hbm(n):
    return [pl.BlockSpec(memory_space=pltpu.HBM) for _ in range(n)]


def forward(plane, vis, cells, count, table, sizes):
    side = plane.shape[0]
    bands = 2 * side // TILE_C
    blocks = cells.shape[0]
    y = (2, bands, side, 256)
    hist = (blocks + 1, 24, 128)
    return pl.pallas_call(
        functools.partial(forward_kernel, sizes[:4]),
        out_shape=[jax.ShapeDtypeStruct(y, bf16), jax.ShapeDtypeStruct(hist, f32)],
        grid_spec=pltpu.PrefetchScalarGridSpec(
            num_scalar_prefetch=1,
            grid=(),
            in_specs=in_hbm(4),
            out_specs=in_hbm(2),
            scratch_shapes=[
                pltpu.VMEM(plane.shape, f32),
                pltpu.VMEM(cells.shape, jnp.int32),
                pltpu.VMEM(vis.shape, f32),
                pltpu.VMEM((sum(sizes[:4]), 128), f32),
                pltpu.VMEM(y, bf16),
                pltpu.VMEM(hist, f32),
                pltpu.VMEM((side, side), bf16),
                pltpu.VMEM((side, side), bf16),
                pltpu.SemaphoreType.DMA((4,)),
                pltpu.SemaphoreType.DMA((2, bands)),
                pltpu.SemaphoreType.DMA((blocks // GROUP,)),
                pltpu.SemaphoreType.DMA,
            ],
        ),
        compiler_params=pltpu.CompilerParams(vmem_limit_bytes=BIG),
        name="forward",
    )(count, plane, cells, vis, table)


def adjoint(entries, bands_of, plane, y, hist, table, sizes):
    _, bands, side, _ = y.shape
    tall = 2 * side // TILE_R
    buffers = [pltpu.VMEM((256, side), bf16), pltpu.VMEM((256, side), bf16), pltpu.VMEM((256, 256), f32)]
    return pl.pallas_call(
        functools.partial(adjoint_kernel, sizes),
        out_shape=jax.ShapeDtypeStruct((side, side), f32),
        grid_spec=pltpu.PrefetchScalarGridSpec(
            num_scalar_prefetch=2,
            grid=(),
            in_specs=in_hbm(4),
            out_specs=whole(1)[0],
            scratch_shapes=[
                pltpu.VMEM(plane.shape, f32),
                pltpu.VMEM(y.shape, bf16),
                pltpu.VMEM(hist.shape, f32),
                pltpu.VMEM(table.shape, f32),
                pltpu.SemaphoreType.DMA((4,)),
                pltpu.VMEM((tall, 16, side), bf16),
                pltpu.VMEM((tall, 16, side), bf16),
                pltpu.VMEM((bands, 256, side), f32),
                pltpu.VMEM((side, side), f32),
                pltpu.VMEM((256, 256), f32),
            ]
            + buffers * 2,
        ),
        compiler_params=pltpu.CompilerParams(vmem_limit_bytes=BIG),
        name="adjoint",
    )(entries, bands_of, plane, y, hist, table)


def halo_kernel(image, edge_rows, up, down):
    channels = up.shape[1]
    rows = image.shape[0] // channels
    for c in range(channels):
        for i in range(2):
            up[i, c : c + 1] = image[(c + 1) * rows - 2 + i : (c + 1) * rows - 1 + i]
            down[i, c : c + 1] = image[c * rows + i : c * rows + i + 1]
    up[2] = edge_rows[1]
    down[2] = edge_rows[0]


def gram_kernel(dual, image, out):
    pick, match = row_maps(dual.shape[0], out.shape[0])
    high, low = split(dual[...] + sigma_step * image[...])
    full = jnp.where(match, nt(high, high) + nt(high, low) + nt(low, high), 0.0)

    def three(x):
        a, rest = split(x)
        b, c = split(x - a.astype(f32))
        return a, b, c

    half = sum(
        lax.dot_general(pick, part, (((0,), (0,)), ((), ())), preferred_element_type=f32)
        for part in three(full)
    )
    out[...] = sum(jnp.dot(part, pick, preferred_element_type=f32) for part in three(half))


def inverse_root(gram, ridge):
    channels = gram.shape[0]
    ci = lax.broadcasted_iota(jnp.int32, (channels, channels), 0)
    cj = lax.broadcasted_iota(jnp.int32, (channels, channels), 1)
    identity = (ci == cj).astype(f32)
    shifted = gram + ridge * identity
    trace = jnp.sum(shifted * identity, keepdims=True)
    current = shifted / trace
    factor = 1.5 * identity - 0.5 * current
    inverse = factor
    for turn in range(1, NS_STEPS):
        current = jnp.dot(current, factor, precision=highest)
        factor = 1.5 * identity - 0.5 * jnp.dot(inverse, current, precision=highest)
        inverse = jnp.dot(factor, inverse, precision=highest)
    return inverse * (math.sqrt(ridge) * lax.rsqrt(trace))


def dual_kernel(ridge, bound, edges, *refs):
    *grams, limit, image, flat_image, up, down = refs[:-19]
    before_in, after_in, dual_in, low_in, wavelet_out, lowrank_out, direction_out = refs[-19:-12]
    before, after, dual, low, wavelet, lowrank, direction, b_hi, b_lo, rims, in_sem, out_sem = refs[-12:]
    reads = [
        pltpu.make_async_copy(source, to, in_sem.at[i])
        for i, (source, to) in enumerate(((low_in, low), (before_in, before), (after_in, after), (dual_in, dual)))
    ]
    for read in reads:
        read.start()
    channels, rows, side = image.shape
    total = channels * rows
    gram = grams[0][...]
    for other in grams[1:]:
        gram = gram + other[...]
    root_hi, root_lo = split(inverse_root(gram, ridge))
    for read in reads:
        read.wait()
    b_hi[...], b_lo[...] = split(low[...] + sigma_step * flat_image[...])
    most = limit[...]

    def rim(middle, inner, outer, held, inside):
        step = columns(middle - 0.5 * (inner + outer))
        return inside * (2.0 * jnp.clip(held + sigma_step * step, -most, most) - held)

    rims[0] = rim(before[1], down[0], before[0], before[2], edges[0])
    rims[1] = rim(after[0], up[1], after[1], after[2], edges[1])
    step_rows = total // PARTS
    step_channels = channels // PARTS
    other, match = row_maps(total, channels)
    match = match[:step_rows]

    def copies(part):
        at = pl.ds(part * step_channels, step_channels)
        pairs = ((direction, direction_out), (wavelet, wavelet_out), (lowrank, lowrank_out))
        return [pltpu.make_async_copy(f.at[at], t.at[at], out_sem.at[i, part]) for i, (f, t) in enumerate(pairs)]

    def one(part, carry):
        pick, _ = row_maps(total, channels, part * step_rows, step_rows)

        def spread(x):
            wide = jnp.dot(pick, x, preferred_element_type=f32).astype(bf16)
            return jnp.where(match, nt(wide, other), 0.0).astype(bf16)

        result = dot3(spread(root_hi), spread(root_lo), b_hi[...], b_lo[...])
        held = low[pl.ds(pl.multiple_of(part * step_rows, step_rows), step_rows), :]
        part_sum = tau_step * (2.0 * result - held)
        for i in range(step_channels):
            c = part * step_channels + i
            at = pl.ds(c, 1)
            w = dual[c]
            b = bound[c]
            step = columns(rows_between(image[c], before[1, at], after[0, at]))
            new = jnp.clip(w + sigma_step * step, -b, b)
            wavelet[c] = new
            detail = columns(rows_between(2.0 * new - w, rims[0, at], rims[1, at]))
            mine = slice(i * rows, (i + 1) * rows)
            lowrank[c] = result[mine]
            direction[c] = part_sum[mine] + tau_step * detail
        for copy in copies(part):
            copy.start()
        return carry

    lax.fori_loop(0, PARTS, one, 0)
    for part in range(PARTS):
        for copy in copies(part):
            copy.wait()


def shift_lanes(x):
    wide = x.shape[-1]
    lane = lax.broadcasted_iota(jnp.int32, x.shape, 1)
    before = jnp.where(lane == 0, 0.0, pltpu.roll(x, 1, 1))
    after = jnp.where(lane == wide - 1, 0.0, pltpu.roll(x, wide - 1, 1))
    return before + after


def columns(x):
    return x - 0.5 * shift_lanes(x)


def rows_between(x, above, below):
    height = x.shape[0]
    row = lax.broadcasted_iota(jnp.int32, x.shape, 0)
    up = jnp.where(row == 0, above, pltpu.roll(x, 1, 0))
    down = jnp.where(row == height - 1, below, pltpu.roll(x, height - 1, 0))
    return x - 0.5 * (up + down)


def row_maps(total, channels, start=0, count=None):
    rows = total // channels
    count = total if count is None else count
    si = lax.broadcasted_iota(jnp.int32, (count, channels), 0) + start
    sj = lax.broadcasted_iota(jnp.int32, (count, channels), 1)
    pick = ((si >= sj * rows) & (si < sj * rows + rows)).astype(f32).astype(bf16)
    i = lax.rem(lax.broadcasted_iota(jnp.int32, (count, 1), 0), rows)
    j = lax.rem(lax.broadcasted_iota(jnp.int32, (1, total), 1), rows)
    return pick, i == j


def halo_rows(image, edge_rows):
    halo = jax.ShapeDtypeStruct((3,) + edge_rows.shape[1:], f32)
    return pl.pallas_call(
        halo_kernel,
        out_shape=[halo, halo],
        in_specs=whole(2),
        out_specs=whole(2),
        compiler_params=pltpu.CompilerParams(vmem_limit_bytes=8 * MIB),
        name="halo",
    )(image, edge_rows)


def local_gram(dual, image, channels):
    return pl.pallas_call(
        gram_kernel,
        out_shape=jax.ShapeDtypeStruct((channels, channels), f32),
        in_specs=whole(2),
        out_specs=whole(1)[0],
        compiler_params=pltpu.CompilerParams(vmem_limit_bytes=12 * MIB),
        name="gram",
    )(dual, image)


def final_kernel(base_in, sent_in, out_ref, base, sent, out, in_sem, out_sem):
    step = base.shape[0] // PARTS

    def reads(part):
        at = pl.ds(part * step, step)
        return [
            pltpu.make_async_copy(f.at[at], t.at[at], in_sem.at[i, part])
            for i, (f, t) in enumerate(((base_in, base), (sent_in, sent)))
        ]

    def write(part):
        at = pl.ds(part * step, step)
        return pltpu.make_async_copy(out.at[at], out_ref.at[at], out_sem.at[part])

    for part in range(PARTS):
        for read in reads(part):
            read.start()
    for part in range(PARTS):
        for read in reads(part):
            read.wait()
        at = slice(part * step, (part + 1) * step)
        out[at] = jnp.maximum(base[at] - sent[at], 0.0)
        write(part).start()
    for part in range(PARTS):
        write(part).wait()


def final_image(base, sent):
    return pl.pallas_call(
        final_kernel,
        out_shape=jax.ShapeDtypeStruct(base.shape, f32),
        in_specs=in_hbm(2),
        out_specs=in_hbm(1)[0],
        scratch_shapes=[pltpu.VMEM(base.shape, f32)] * 3
        + [pltpu.SemaphoreType.DMA((2, PARTS)), pltpu.SemaphoreType.DMA((PARTS,))],
        compiler_params=pltpu.CompilerParams(vmem_limit_bytes=8 * MIB),
        name="final",
    )(base, sent)


def dual_update(ridge, bound, edges, grams, image, up, down, before, after, dual, low):
    channels, rows, side = image.shape
    flat = (channels * rows, side)
    smem = pl.BlockSpec(memory_space=pltpu.SMEM)
    return pl.pallas_call(
        functools.partial(dual_kernel, ridge),
        out_shape=[jax.ShapeDtypeStruct(image.shape, f32)] * 3,
        in_specs=[smem, smem] + whole(len(grams) + 5) + in_hbm(4),
        out_specs=in_hbm(3),
        scratch_shapes=[
            pltpu.VMEM(before.shape, f32),
            pltpu.VMEM(after.shape, f32),
            pltpu.VMEM(image.shape, f32),
            pltpu.VMEM(flat, f32),
            pltpu.VMEM(image.shape, f32),
            pltpu.VMEM(image.shape, f32),
            pltpu.VMEM(image.shape, f32),
            pltpu.VMEM(flat, bf16),
            pltpu.VMEM(flat, bf16),
            pltpu.VMEM((2, channels, side), f32),
            pltpu.SemaphoreType.DMA((4,)),
            pltpu.SemaphoreType.DMA((3, PARTS)),
        ],
        compiler_params=pltpu.CompilerParams(vmem_limit_bytes=24 * MIB),
        name="dual",
    )(bound, edges, *grams, bound[:, None], image, image.reshape(flat), up, down, before, after, dual, low.reshape(flat))


def per_device(
    image, visibilities, tile_index, cells, block_count, lowrank_dual, wavelet_dual, wavelet_bound
):
    side = image.shape[-1]
    channels, rows_here, _ = lowrank_dual.shape
    devices = lax.axis_size(RING)
    pieces = lax.axis_size("pix")
    here = lax.axis_index(RING)
    flat = (channels * rows_here, side)

    facet_image = lax.all_to_all(
        image.reshape(devices, rows_here, side), RING, split_axis=0, concat_axis=0, tiled=True
    )

    bands = 2 * side // TILE_C
    chunks = tile_index.shape[1] // GROUP + bands + 1
    table, sizes = small_tables(side, side)
    table = jnp.asarray(table)
    entries, bands_of = plan_blocks(tile_index[0], block_count[0], bands, chunks)
    y, hist = forward(image[0], visibilities[:, 0], cells[0], block_count, table, sizes)
    edge_rows = jnp.stack([wavelet_dual[:, 0], wavelet_dual[:, -1]])
    edges = jnp.stack([here > 0, here < devices - 1]).astype(f32)
    facet_image, y, entries, bands_of, edge_rows, edges = lax.optimization_barrier(
        (facet_image, y, entries, bands_of, edge_rows, edges)
    )

    up, down = halo_rows(facet_image.reshape(flat), edge_rows)
    ahead = [(i, i + 1) for i in range(devices - 1)]
    before = lax.ppermute(up, RING, ahead)
    after = lax.ppermute(down, RING, [(j, i) for i, j in ahead])
    gram = local_gram(lowrank_dual.reshape(flat), facet_image.reshape(flat), channels)
    grams = [gram] + [
        lax.ppermute(gram, "pix", [(i, (i + s) % pieces) for i in range(pieces)]) for s in range(1, pieces)
    ]
    ridge = float(rows_here * side * pieces)
    wavelet_next, lowrank_next, direction = dual_update(
        ridge, wavelet_bound, edges, grams, facet_image, up, down, before, after, wavelet_dual, lowrank_dual
    )
    direction, y = lax.optimization_barrier((direction, y))
    returned = lax.all_to_all(direction, RING, split_axis=0, concat_axis=0, tiled=True)
    base = adjoint(entries, bands_of, image[0], y, hist, table, sizes)
    image_next = final_image(base, returned.reshape(side, side))
    return (image_next[None], lowrank_next, wavelet_next)


def solution(mesh):
    return jax.shard_map(
        per_device,
        mesh=mesh,
        in_specs=(
            P(RING, None, None),
            P(None, RING, None, None),
            P(RING, None),
            P(RING, None, None),
            P(RING),
            P(None, RING, None),
            P(None, RING, None),
            P(),
        ),
        out_specs=(P(RING, None, None), P(None, RING, None), P(None, RING, None)),
        check_vma=False,
    )
```

time: 117 us -> 92.5 us (0.79)
  starting transfers between devices: 37.6 us -> 19.8 us
  waiting for transfers between devices: 7.37 us -> 22.8 us
  Pallas kernels: 54.2 us -> 40.9 us
  other arithmetic: 12.4 us -> 4.14 us
    pallas_call x3 -> x5, Pallas kernels: 50.4 us -> 39.2 us  [the longest x1 18.5 us: adjoint(): pl.pallas_call(functools.partial(adjoint_kernel, sizes), out_shape=jax.Sh...]
    all_to_all x1, waiting for transfers between devices: 0.01 us -> 9.7 us  [per_device(): lax.all_to_all(image.reshape(devices, rows_here, side), RING, split_axis=...]
    ppermute x4 -> x2, starting transfers between devices: 14.7 us -> 7.35 us  [the longest x1 5.44 us: per_device(): after = lax.ppermute(down, RING, [(j, i) for i, j in ahead])]
    ppermute x3, starting transfers between devices: 7.25 us -> 1.51 us  [per_device(): lax.ppermute(gram, 'pix', [(i, (i + s) % pieces) for i in range(pieces)])]
    ppermute x3, waiting for transfers between devices: 0.01 us -> 5.03 us  [per_device(): lax.ppermute(gram, 'pix', [(i, (i + s) % pieces) for i in range(pieces)])]
    all_to_all x1, starting transfers between devices: 8.51 us -> 3.83 us  [per_device(): lax.all_to_all(direction, RING, split_axis=0, concat_axis=0, tiled=True)]
    sub x3 -> x0, other arithmetic: 4.42 us -> none  [the longest x2 2.84 us: row_difference(): return rimmed[:, 1:-1] - 0.5 * (rimmed[:, :-2] + rimmed[:, 2:])]
    max x1 -> x0, other arithmetic: 2.88 us -> none  [per_device(): image_next = jnp.maximum(image[0] - tau_step * (gradient + returned), 0.0)]
  transfers between devices with their start and end apart: 9 -> 7, of which waited for: 1 -> 4; matrix products, arithmetic and copies ran while one was open for 8% -> 5% of each run, Pallas kernels for 38% -> 34%
where the time goes in v1:
time: 92.5 us; the launch traced here: 92 us
  Pallas kernels  40.9 us (44%)
  waiting for transfers between devices  22.8 us (25%)
  starting transfers between devices  19.8 us (21%)
  other arithmetic  4.14 us (4%)
  local copies, waits for them, and re-layouts  3.02 us (3%)
  between operations  1.46 us (2%)
    pallas_call x1, Pallas kernels, adjoint(): pl.pallas_call(functools.partial(adjoint_kernel, sizes), out_shape=jax.Sh...  18.5 us
    pallas_call x1, Pallas kernels, forward(): pl.pallas_call(functools.partial(forward_kernel, sizes[:4]), out_shape=[j...  11.1 us
    all_to_all x1, waiting for transfers between devices, per_device(): lax.all_to_all(image.reshape(devices, rows_here, side), RING, split_axis=...  9.7 us
    all_to_all x1, waiting for transfers between devices, per_device(): lax.all_to_all(direction, RING, split_axis=0, concat_axis=0, tiled=True)  8.02 us
    pallas_call x1, Pallas kernels, dual_update(): pl.pallas_call(functools.partial(dual_kernel, ridge), out_shape=[jax.Shap...  7.63 us
    all_to_all x1, starting transfers between devices, per_device(): lax.all_to_all(image.reshape(devices, rows_here, side), RING, split_axis=...  7.1 us
    ppermute x1, starting transfers between devices, per_device(): after = lax.ppermute(down, RING, [(j, i) for i, j in ahead])  5.44 us
    ppermute x3, waiting for transfers between devices, per_device(): lax.ppermute(gram, 'pix', [(i, (i + s) % pieces) for i in range(pieces)])  5.03 us
  transfers between devices with their start and end apart: 7, of which 4 were waited for; matrix products, arithmetic and copies ran while one was open for 5% of the time, Pallas kernels for 34%

profile of v1, /device:TPU:1, one launch (start us, length us, event | category | flops | bytes accessed | tf_op | source)
XLA Modules:
  0.0 92.0 jit_solution(10620826910172611820)
XLA Ops:
  0.6 0.0 copy-start.2
  0.6 0.0 copy-start.1
  0.7 0.0 copy-start.4
  0.7 7.1 %all-to-all-start = ((f32[32,16,512]{2,1,0:T(8,128)}), f32[32,16,512]{2,1,0:T(8,128)S(1)}, u32[]{:S(2)}, u32[]{:S(2)}) async-start(f32[32,16,512]{2,1,0:T(8,128)} %bitcast.30), calls=%async_computation | async-start | bytes 2097152 | tf_op jit(solution)/shard_map/all_to_all | solution.py:599
  8.4 0.7 compare_select_fusion.1
  9.1 0.1 convert_reduce_fusion.1
  9.2 0.1 select_reduce_fusion.2
  9.4 0.7 compare_select_fusion.7
  10.1 0.6 slice.9
  10.7 0.1 select_reduce_fusion.1
  10.7 0.2 convert_reduce_fusion
  10.9 11.1 %forward.1 = (bf16[2,8,512,256]{3,2,1,0:T(8,128)(2,1)}, f32[257,24,128]{2,1,0:T(8,128)}) custom-call(s32[1]{0:T(128)} %copy.22.live, f32[512,512]{1,0:T(8,128)} %bitcast.31, s32[256,128]{1,0:T(8,128)} %bitcast.35, f32[2,256,128]{2,1,0:T(8,128)} %bitcast.34, f32[1472,128]{1,0:T(8,128)} %constant.74.clone.table_in), custom_call_target="tpu_custom_call" | custom-call | tf_op jit(solution)/shard_map/forward/pallas_call | solution.py:294
  22.0 0.1 add_convert_fusion.edges
  22.1 0.1 convert_reduce_fusion.2
  22.2 1.3 %pad_add_fusion.bands_of = s32[26]{0:T(128)} fusion(s32[1]{0:T(128)} %slice.9, s32[25]{0:T(128)S(1)} %broadcast_minimum_fusion), kind=kLoop, calls=%fused_computation.35 | loop fusion | flops 26 | bytes 208 | tf_op jit(solution)/shard_map/concatenate | solution.py:100
  23.5 0.0 copy-done.2
  23.5 0.1 fusion.2
  23.7 0.1 select_reduce_fusion
  23.8 0.6 broadcast_add_fusion.entries
  24.4 9.7 %all-to-all-done.refs_5_ = f32[32,16,512]{2,1,0:T(8,128)S(1)} async-done(((f32[32,16,512]{2,1,0:T(8,128)}), f32[32,16,512]{2,1,0:T(8,128)S(1)}, u32[]{:S(2)}, u32[]{:S(2)}) %all-to-all-start) | async-done | bytes 1048608 | tf_op jit(solution)/shard_map/all_to_all | solution.py:599
  34.1 0.8 halo.1
  34.9 1.9 %collective-permute-start.3 = (f32[3,32,512]{2,1,0:T(8,128)S(1)}, f32[3,32,512]{2,1,0:T(8,128)}, u32[]{:S(2)}, u32[]{:S(2)}) collective-permute-start(f32[3,32,512]{2,1,0:T(8,128)S(1)} %get-tuple-element.24.refs_7_), channel_id=1, source_target_pairs={{0,1},{1,2},{2,3},{3,4},{4,5},{5,6},{6,7},{7,8},{8,9},{9,10},{10,1... | collective-permute-start | bytes 589832 | tf_op jit(solution)/shard_map/ppermute | solution.py:617
  36.8 5.4 %collective-permute-start.4 = (f32[3,32,512]{2,1,0:T(8,128)}, f32[3,32,512]{2,1,0:T(8,128)}, u32[]{:S(2)}, u32[]{:S(2)}) collective-permute-start(f32[3,32,512]{2,1,0:T(8,128)} %get-tuple-element.25.refs_8_), channel_id=1, source_target_pairs={{1,0},{2,1},{3,2},{4,3},{5,4},{6,5},{7,6},{8,7},{9,8},{10,9},{11,1... | collective-permute-start | bytes 589832 | tf_op jit(solution)/shard_map/ppermute | solution.py:618
  42.2 0.0 copy-done.1
  42.3 1.7 %gram.1.refs_0_ = f32[32,32]{1,0:T(8,128)S(1)} custom-call(f32[512,512]{1,0:T(8,128)S(1)} %bitcast.27, f32[512,512]{1,0:T(8,128)S(1)} %bitcast.24), custom_call_target="tpu_custom_call" | custom-call | tf_op jit(solution)/shard_map/gram/pallas_call | solution.py:511
  43.9 0.1 collective-permute-start.2
  44.0 0.1 collective-permute-start.1
  44.1 1.4 %collective-permute-start = (f32[32,32]{1,0:T(8,128)S(1)}, f32[32,32]{1,0:T(8,128)S(1)}, u32[]{:S(2)}, u32[]{:S(2)}) collective-permute-start(f32[32,32]{1,0:T(8,128)S(1)} %gram.1.refs_0_), channel_id=1, source_target_pairs={{0,1},{1,2},{2,3},{3,0},{4,5},{5,6},{6,7},{7,4},{8,9},{9,10},{10,1... | collective-permute-start | bytes 12296 | tf_op jit(solution)/shard_map/ppermute | solution.py:621
  45.5 0.0 copy-done.4
  45.5 0.1 copy.17.refs_4_
  45.5 4.3 %collective-permute-done.2.refs_3_ = f32[32,32]{1,0:T(8,128)S(1)} collective-permute-done((f32[32,32]{1,0:T(8,128)S(1)}, f32[32,32]{1,0:T(8,128)S(1)}, u32[]{:S(2)}, u32[]{:S(2)}) %collective-permute-start.2) | collective-permute-done | bytes 4128 | tf_op jit(solution)/shard_map/ppermute | solution.py:621
  49.9 0.7 collective-permute-done.1.refs_2_
  50.6 0.0 collective-permute-done.refs_1_
  50.6 0.0 collective-permute-done.3.refs_9_
  50.6 0.0 collective-permute-done.4.refs_10_
  50.6 7.6 %dual.1 = (f32[32,16,512]{2,1,0:T(8,128)}, f32[32,16,512]{2,1,0:T(8,128)}, f32[32,16,512]{2,1,0:T(8,128)S(1)}) custom-call(f32[32]{0:T(128)S(1)} %copy-done.4, f32[2]{0:T(128)S(1)} %add_convert_fusion.edges, f32[32,32]{1,0:T(8,128)S(1)} %gram.1.refs_0_, f32[32,32]{1,0:T(8,128)S(1)} %collective-permute-done.refs_1_, ...), custom_call_target="tpu_custom_call" | custom-call | tf_op jit(solution)/shard_map/dual/pallas_call | solution.py:565
  58.2 0.0 copy-start.3
  58.2 1.0 %copy-done.3 = f32[32,16,512]{2,1,0:T(8,128)} copy-done((f32[32,16,512]{2,1,0:T(8,128)}, f32[32,16,512]{2,1,0:T(8,128)S(1)}, u32[]{:S(2)}) %copy-start.3) | copy-done | bytes 1048600
  59.2 3.8 %all-to-all-start.1 = ((f32[32,16,512]{2,1,0:T(8,128)}), f32[32,16,512]{2,1,0:T(8,128)S(1)}, u32[]{:S(2)}, u32[]{:S(2)}) async-start(f32[32,16,512]{2,1,0:T(8,128)} %copy-done.3), calls=%async_computation.1 | async-start | bytes 2097152 | tf_op jit(solution)/shard_map/all_to_all | solution.py:628
  63.1 18.5 %adjoint.1.base_in = f32[512,512]{1,0:T(8,128)} custom-call(s32[400]{0:T(512)} %broadcast_add_fusion.entries, s32[26]{0:T(128)} %pad_add_fusion.bands_of, f32[512,512]{1,0:T(8,128)} %bitcast.32, bf16[2,8,512,256]{3,2,1,0:T(8,128)(2,1)} %get-tuple-element.28.y_in, f32[257,24,128]{2,1,0:T(8,128)} %get-tuple-element.29.hist_in, f32[1472,128]{1,0:T(8,128)} %constant.74.clone.table_in), custom_call_target="tpu_custom_call" | custom-call | tf_op jit(solution)/shard_map/adjoint/pallas_call | solution.py:326
  81.5 8.0 %all-to-all-done.1 = f32[32,16,512]{2,1,0:T(8,128)S(1)} async-done(((f32[32,16,512]{2,1,0:T(8,128)}), f32[32,16,512]{2,1,0:T(8,128)S(1)}, u32[]{:S(2)}, u32[]{:S(2)}) %all-to-all-start.1) | async-done | bytes 1048608 | tf_op jit(solution)/shard_map/all_to_all | solution.py:628
  89.6 0.0 copy-start
  89.6 1.2 %copy-done = f32[512,512]{1,0:T(8,128)S(1)} copy-done((f32[512,512]{1,0:T(8,128)S(1)}, f32[512,512]{1,0:T(8,128)}, u32[]{:S(2)}) %copy-start) | copy-done | bytes 1048600
  90.8 1.2 %final.1 = f32[512,512]{1,0:T(8,128)} custom-call(f32[512,512]{1,0:T(8,128)S(1)} %copy-done, f32[512,512]{1,0:T(8,128)S(1)} %bitcast.26), custom_call_target="tpu_custom_call" | custom-call | tf_op jit(solution)/shard_map/final/pallas_call | solution.py:549
  (7 shorter events, 0.1 us)
Async XLA Ops:
  0.6 22.9 %copy-start.2 = (f32[32,16,512]{2,1,0:T(8,128)S(1)}, f32[32,16,512]{2,1,0:T(8,128)}, u32[]{:S(2)}) copy-start(f32[32,16,512]{2,1,0:T(8,128)} %refs_11_.1) | copy-start | bytes 3145732
  0.6 41.6 %copy-start.1 = (f32[32,16,512]{2,1,0:T(8,128)S(1)}, f32[32,16,512]{2,1,0:T(8,128)}, u32[]{:S(2)}) copy-start(f32[32,16,512]{2,1,0:T(8,128)} %param.14) | copy-start | bytes 3145732
  0.7 44.8 %copy-start.4 = (f32[32]{0:T(128)S(1)}, f32[32]{0:T(128)}, u32[]{:S(2)}) copy-start(f32[32]{0:T(128)} %bound.1) | copy-start | bytes 388
  0.7 33.5 %all-to-all-start = ((f32[32,16,512]{2,1,0:T(8,128)}), f32[32,16,512]{2,1,0:T(8,128)S(1)}, u32[]{:S(2)}, u32[]{:S(2)}) async-start(f32[32,16,512]{2,1,0:T(8,128)} %bitcast.30), calls=%async_computation | async-start | bytes 2097152 | tf_op jit(solution)/shard_map/all_to_all | solution.py:599
  34.9 15.7 %collective-permute-start.3 = (f32[3,32,512]{2,1,0:T(8,128)S(1)}, f32[3,32,512]{2,1,0:T(8,128)}, u32[]{:S(2)}, u32[]{:S(2)}) collective-permute-start(f32[3,32,512]{2,1,0:T(8,128)S(1)} %get-tuple-element.24.refs_7_), channel_id=1, source_target_pairs={{0,1},{1,2},{2,3},{3,4},{4,5},{5,6},{6,7},{7,8},{8,9},{9,10},{10,1... | collective-permute-start | bytes 589832 | tf_op jit(solution)/shard_map/ppermute | solution.py:617
  36.8 13.8 %collective-permute-start.4 = (f32[3,32,512]{2,1,0:T(8,128)}, f32[3,32,512]{2,1,0:T(8,128)}, u32[]{:S(2)}, u32[]{:S(2)}) collective-permute-start(f32[3,32,512]{2,1,0:T(8,128)} %get-tuple-element.25.refs_8_), channel_id=1, source_target_pairs={{1,0},{2,1},{3,2},{4,3},{5,4},{6,5},{7,6},{8,7},{9,8},{10,9},{11,1... | collective-permute-start | bytes 589832 | tf_op jit(solution)/shard_map/ppermute | solution.py:618
  43.9 5.9 %collective-permute-start.2 = (f32[32,32]{1,0:T(8,128)S(1)}, f32[32,32]{1,0:T(8,128)S(1)}, u32[]{:S(2)}, u32[]{:S(2)}) collective-permute-start(f32[32,32]{1,0:T(8,128)S(1)} %gram.1.refs_0_), channel_id=1, source_target_pairs={{0,3},{1,0},{2,1},{3,2},{4,7},{5,4},{6,5},{7,6},{8,11},{9,8},{10,9... | collective-permute-start | bytes 12296 | tf_op jit(solution)/shard_map/ppermute | solution.py:621
  44.0 6.6 %collective-permute-start.1 = (f32[32,32]{1,0:T(8,128)S(1)}, f32[32,32]{1,0:T(8,128)S(1)}, u32[]{:S(2)}, u32[]{:S(2)}) collective-permute-start(f32[32,32]{1,0:T(8,128)S(1)} %gram.1.refs_0_), channel_id=1, source_target_pairs={{0,2},{1,3},{2,0},{3,1},{4,6},{5,7},{6,4},{7,5},{8,10},{9,11},{10,... | collective-permute-start | bytes 12296 | tf_op jit(solution)/shard_map/ppermute | solution.py:621
  44.1 6.5 %collective-permute-start = (f32[32,32]{1,0:T(8,128)S(1)}, f32[32,32]{1,0:T(8,128)S(1)}, u32[]{:S(2)}, u32[]{:S(2)}) collective-permute-start(f32[32,32]{1,0:T(8,128)S(1)} %gram.1.refs_0_), channel_id=1, source_target_pairs={{0,1},{1,2},{2,3},{3,0},{4,5},{5,6},{6,7},{7,4},{8,9},{9,10},{10,1... | collective-permute-start | bytes 12296 | tf_op jit(solution)/shard_map/ppermute | solution.py:621
  58.2 1.0 %copy-start.3 = (f32[32,16,512]{2,1,0:T(8,128)}, f32[32,16,512]{2,1,0:T(8,128)S(1)}, u32[]{:S(2)}) copy-start(f32[32,16,512]{2,1,0:T(8,128)S(1)} %get-tuple-element.30) | copy-start | bytes 3145732
  59.2 30.3 %all-to-all-start.1 = ((f32[32,16,512]{2,1,0:T(8,128)}), f32[32,16,512]{2,1,0:T(8,128)S(1)}, u32[]{:S(2)}, u32[]{:S(2)}) async-start(f32[32,16,512]{2,1,0:T(8,128)} %copy-done.3), calls=%async_computation.1 | async-start | bytes 2097152 | tf_op jit(solution)/shard_map/all_to_all | solution.py:628
  89.6 1.2 %copy-start = (f32[512,512]{1,0:T(8,128)S(1)}, f32[512,512]{1,0:T(8,128)}, u32[]{:S(2)}) copy-start(f32[512,512]{1,0:T(8,128)} %adjoint.1.base_in) | copy-start | bytes 3145732

commit v2 on v1

--- a/solution.py
+++ b/solution.py
@@ -14,6 +14,7 @@
 NS_STEPS = 5
 GROUP = 16
 PARTS = 4
+HALVES = 1
 RING = ("facet", "pix")
 
 highest = lax.Precision.HIGHEST
@@ -350,19 +351,15 @@
     )(entries, bands_of, plane, y, hist, table)
 
 
-def halo_kernel(image, edge_rows, up, down):
-    channels = up.shape[1]
+def gram_kernel(even, dual, image, first, second):
+    channels, side = second.shape
     rows = image.shape[0] // channels
+    left, right = jnp.where(even[0] == 1, rows - 1, 0), jnp.where(even[0] == 1, 0, rows - 1)
     for c in range(channels):
-        for i in range(2):
-            up[i, c : c + 1] = image[(c + 1) * rows - 2 + i : (c + 1) * rows - 1 + i]
-            down[i, c : c + 1] = image[c * rows + i : c * rows + i + 1]
-    up[2] = edge_rows[1]
-    down[2] = edge_rows[0]
-
-
-def gram_kernel(dual, image, out):
-    pick, match = row_maps(dual.shape[0], out.shape[0])
+        first[c : c + 1, :side] = image[pl.ds(c * rows + left, 1), :]
+        second[c : c + 1] = image[pl.ds(c * rows + right, 1), :]
+    first[:, side:] = jnp.zeros((channels, first.shape[1] - side), f32)
+    pick, match = row_maps(dual.shape[0], channels)
     high, low = split(dual[...] + sigma_step * image[...])
     full = jnp.where(match, nt(high, high) + nt(high, low) + nt(low, high), 0.0)
 
@@ -375,11 +372,51 @@
         lax.dot_general(pick, part, (((0,), (0,)), ((), ())), preferred_element_type=f32)
         for part in three(full)
     )
-    out[...] = sum(jnp.dot(part, pick, preferred_element_type=f32) for part in three(half))
-
-
-def inverse_root(gram, ridge):
-    channels = gram.shape[0]
+    first[:, side : side + channels] = sum(jnp.dot(part, pick, preferred_element_type=f32) for part in three(half))
+
+
+def packing(rows, side):
+    short = 8 if rows % 8 == 0 else rows
+    return short, rows // short * side, 2 * side // short
+
+
+def dual_kernel(ridge, bound, even, *refs):
+    *grams, image, flat_image, first, second, dual, low = refs[:-11]
+    wavelet_out, lowrank_out, packed_out = refs[-11:-8]
+    wavelet, lowrank, packed, beside, b_hi, b_lo, result, out_sem = refs[-8:]
+    channels, rows, side = image.shape
+    short, wide, spare = packing(rows, side)
+    total = channels * rows
+    step_rows = total // PARTS
+    step_channels = channels // PARTS
+    one_way, other_way = first[:, :side], second[...]
+    beside[0] = jnp.where(even[0] == 1, other_way, one_way)
+    beside[1] = jnp.where(even[0] == 1, one_way, other_way)
+
+    def copy(which, part):
+        source, to = ((packed, packed_out), (wavelet, wavelet_out), (lowrank, lowrank_out))[which]
+        at = pl.ds(part * step_channels, step_channels)
+        return pltpu.make_async_copy(source.at[at], to.at[at], out_sem.at[which, part])
+
+    def details(part):
+        for c in range(part * step_channels, (part + 1) * step_channels):
+            w = dual[c]
+            b = bound[c]
+            step = columns(rows_between(image[c], beside[0, c : c + 1], beside[1, c : c + 1]))
+            new = jnp.clip(w + sigma_step * step, -b, b)
+            wavelet[c] = new
+            slope = columns(tau_step * (2.0 * new - w))
+            own = rows_between(slope, 0.0, 0.0)
+            for h in range(rows // short):
+                packed[c, :, h * side : (h + 1) * side] = own[h * short : (h + 1) * short]
+            for k in range(short // 2):
+                lanes = slice(k * spare, (k + 1) * spare)
+                packed[c, k : k + 1, wide:] = -0.5 * slope[:1, lanes]
+                packed[c, short // 2 + k : short // 2 + k + 1, wide:] = -0.5 * slope[rows - 1 :, lanes]
+
+    gram = grams[0][...]
+    for other in grams[1:]:
+        gram = gram + other[...]
     ci = lax.broadcasted_iota(jnp.int32, (channels, channels), 0)
     cj = lax.broadcasted_iota(jnp.int32, (channels, channels), 1)
     identity = (ci == cj).astype(f32)
@@ -390,78 +427,39 @@
     inverse = factor
     for turn in range(1, NS_STEPS):
         current = jnp.dot(current, factor, precision=highest)
+        if turn <= PARTS:
+            details(turn - 1)
         factor = 1.5 * identity - 0.5 * jnp.dot(inverse, current, precision=highest)
         inverse = jnp.dot(factor, inverse, precision=highest)
-    return inverse * (math.sqrt(ridge) * lax.rsqrt(trace))
-
-
-def dual_kernel(ridge, bound, edges, *refs):
-    *grams, limit, image, flat_image, up, down = refs[:-19]
-    before_in, after_in, dual_in, low_in, wavelet_out, lowrank_out, direction_out = refs[-19:-12]
-    before, after, dual, low, wavelet, lowrank, direction, b_hi, b_lo, rims, in_sem, out_sem = refs[-12:]
-    reads = [
-        pltpu.make_async_copy(source, to, in_sem.at[i])
-        for i, (source, to) in enumerate(((low_in, low), (before_in, before), (after_in, after), (dual_in, dual)))
-    ]
-    for read in reads:
-        read.start()
-    channels, rows, side = image.shape
-    total = channels * rows
-    gram = grams[0][...]
-    for other in grams[1:]:
-        gram = gram + other[...]
-    root_hi, root_lo = split(inverse_root(gram, ridge))
-    for read in reads:
-        read.wait()
+    for part in range(NS_STEPS - 1, PARTS):
+        details(part)
+    for part in range(PARTS):
+        copy(1, part).start()
+    root_hi, root_lo = split(inverse * (math.sqrt(ridge) * lax.rsqrt(trace)))
     b_hi[...], b_lo[...] = split(low[...] + sigma_step * flat_image[...])
-    most = limit[...]
-
-    def rim(middle, inner, outer, held, inside):
-        step = columns(middle - 0.5 * (inner + outer))
-        return inside * (2.0 * jnp.clip(held + sigma_step * step, -most, most) - held)
-
-    rims[0] = rim(before[1], down[0], before[0], before[2], edges[0])
-    rims[1] = rim(after[0], up[1], after[1], after[2], edges[1])
-    step_rows = total // PARTS
-    step_channels = channels // PARTS
-    other, match = row_maps(total, channels)
-    match = match[:step_rows]
-
-    def copies(part):
-        at = pl.ds(part * step_channels, step_channels)
-        pairs = ((direction, direction_out), (wavelet, wavelet_out), (lowrank, lowrank_out))
-        return [pltpu.make_async_copy(f.at[at], t.at[at], out_sem.at[i, part]) for i, (f, t) in enumerate(pairs)]
-
-    def one(part, carry):
-        pick, _ = row_maps(total, channels, part * step_rows, step_rows)
+    pick, match = row_maps(total, channels)
+    half = total // HALVES
+
+    for h in range(HALVES):
+        at = slice(h * half, (h + 1) * half)
 
         def spread(x):
-            wide = jnp.dot(pick, x, preferred_element_type=f32).astype(bf16)
-            return jnp.where(match, nt(wide, other), 0.0).astype(bf16)
-
-        result = dot3(spread(root_hi), spread(root_lo), b_hi[...], b_lo[...])
-        held = low[pl.ds(pl.multiple_of(part * step_rows, step_rows), step_rows), :]
-        part_sum = tau_step * (2.0 * result - held)
-        for i in range(step_channels):
-            c = part * step_channels + i
-            at = pl.ds(c, 1)
-            w = dual[c]
-            b = bound[c]
-            step = columns(rows_between(image[c], before[1, at], after[0, at]))
-            new = jnp.clip(w + sigma_step * step, -b, b)
-            wavelet[c] = new
-            detail = columns(rows_between(2.0 * new - w, rims[0, at], rims[1, at]))
-            mine = slice(i * rows, (i + 1) * rows)
-            lowrank[c] = result[mine]
-            direction[c] = part_sum[mine] + tau_step * detail
-        for copy in copies(part):
-            copy.start()
-        return carry
-
-    lax.fori_loop(0, PARTS, one, 0)
-    for part in range(PARTS):
-        for copy in copies(part):
-            copy.wait()
+            narrow = jnp.dot(pick[at], x, preferred_element_type=f32).astype(bf16)
+            return jnp.where(match[at], nt(narrow, pick), 0.0).astype(bf16)
+
+        result[...] = dot3(spread(root_hi), spread(root_lo), b_hi[...], b_lo[...])
+        for part in range(h * PARTS // HALVES, (h + 1) * PARTS // HALVES):
+            for c in range(part * step_channels, (part + 1) * step_channels):
+                mine = result[c * rows - h * half : (c + 1) * rows - h * half]
+                lowrank[c] = mine
+                more = tau_step * (2.0 * mine - low[c * rows : (c + 1) * rows])
+                for i in range(rows // short):
+                    packed[c, :, i * side : (i + 1) * side] += more[i * short : (i + 1) * short]
+            copy(0, part).start()
+            copy(2, part).start()
+    for which in range(3):
+        for part in range(PARTS):
+            copy(which, part).wait()
 
 
 def shift_lanes(x):
@@ -495,51 +493,61 @@
     return pick, i == j
 
 
-def halo_rows(image, edge_rows):
-    halo = jax.ShapeDtypeStruct((3,) + edge_rows.shape[1:], f32)
-    return pl.pallas_call(
-        halo_kernel,
-        out_shape=[halo, halo],
-        in_specs=whole(2),
-        out_specs=whole(2),
-        compiler_params=pltpu.CompilerParams(vmem_limit_bytes=8 * MIB),
-        name="halo",
-    )(image, edge_rows)
-
-
-def local_gram(dual, image, channels):
+def local_gram(even, dual, image, channels):
+    side = image.shape[1]
+    lanes = side + -(-channels // 128) * 128
     return pl.pallas_call(
         gram_kernel,
-        out_shape=jax.ShapeDtypeStruct((channels, channels), f32),
-        in_specs=whole(2),
-        out_specs=whole(1)[0],
+        out_shape=[jax.ShapeDtypeStruct((channels, n), f32) for n in (lanes, side)],
+        in_specs=[pl.BlockSpec(memory_space=pltpu.SMEM)] + whole(2),
+        out_specs=whole(2),
         compiler_params=pltpu.CompilerParams(vmem_limit_bytes=12 * MIB),
         name="gram",
-    )(dual, image)
-
-
-def final_kernel(base_in, sent_in, out_ref, base, sent, out, in_sem, out_sem):
-    step = base.shape[0] // PARTS
+    )(even, dual, image)
+
+
+def final_kernel(base_in, sent_in, out_ref, base, sent, out, base_sem, sent_sem, out_sem):
+    devices, short, lanes = sent.shape
+    side = base.shape[1]
+    rows = base.shape[0] // devices
+    _, wide, spare = packing(rows, side)
+    step = devices // PARTS
 
     def reads(part):
-        at = pl.ds(part * step, step)
-        return [
-            pltpu.make_async_copy(f.at[at], t.at[at], in_sem.at[i, part])
-            for i, (f, t) in enumerate(((base_in, base), (sent_in, sent)))
-        ]
+        at, to = pl.ds(part * step * rows, step * rows), pl.ds(part * step, step)
+        return (
+            pltpu.make_async_copy(base_in.at[at], base.at[at], base_sem.at[part]),
+            pltpu.make_async_copy(sent_in.at[to], sent.at[to], sent_sem.at[part]),
+        )
 
     def write(part):
-        at = pl.ds(part * step, step)
+        at = pl.ds(part * step * rows, step * rows)
         return pltpu.make_async_copy(out.at[at], out_ref.at[at], out_sem.at[part])
+
+    def beside(d, first):
+        return jnp.concatenate([sent[d, first + k : first + k + 1, wide:] for k in range(short // 2)], axis=1)
+
+    def wait(part):
+        for read in reads(part):
+            read.wait()
 
     for part in range(PARTS):
         for read in reads(part):
             read.start()
+    wait(0)
+    row = lax.broadcasted_iota(jnp.int32, (short, side), 0)
     for part in range(PARTS):
-        for read in reads(part):
-            read.wait()
-        at = slice(part * step, (part + 1) * step)
-        out[at] = jnp.maximum(base[at] - sent[at], 0.0)
+        if part + 1 < PARTS:
+            wait(part + 1)
+        for d in range(part * step, (part + 1) * step):
+            for h in range(rows // short):
+                at = slice(d * rows + h * short, d * rows + (h + 1) * short)
+                left = base[at] - sent[d, :, h * side : (h + 1) * side]
+                if h == 0 and d > 0:
+                    left = jnp.where(row == 0, left - beside(d - 1, short // 2), left)
+                if (h + 1) * short == rows and d + 1 < devices:
+                    left = jnp.where(row == short - 1, left - beside(d + 1, 0), left)
+                out[at] = jnp.maximum(left, 0.0)
         write(part).start()
     for part in range(PARTS):
         write(part).wait()
@@ -551,39 +559,42 @@
         out_shape=jax.ShapeDtypeStruct(base.shape, f32),
         in_specs=in_hbm(2),
         out_specs=in_hbm(1)[0],
-        scratch_shapes=[pltpu.VMEM(base.shape, f32)] * 3
-        + [pltpu.SemaphoreType.DMA((2, PARTS)), pltpu.SemaphoreType.DMA((PARTS,))],
+        scratch_shapes=[
+            pltpu.VMEM(base.shape, f32),
+            pltpu.VMEM(sent.shape, f32),
+            pltpu.VMEM(base.shape, f32),
+        ]
+        + [pltpu.SemaphoreType.DMA((PARTS,))] * 3,
+        input_output_aliases={0: 0},
         compiler_params=pltpu.CompilerParams(vmem_limit_bytes=8 * MIB),
         name="final",
     )(base, sent)
 
 
-def dual_update(ridge, bound, edges, grams, image, up, down, before, after, dual, low):
+def dual_update(ridge, bound, even, grams, image, first, second, dual, low):
     channels, rows, side = image.shape
     flat = (channels * rows, side)
+    short, wide, spare = packing(rows, side)
+    packed = (channels, short, wide + spare)
     smem = pl.BlockSpec(memory_space=pltpu.SMEM)
     return pl.pallas_call(
         functools.partial(dual_kernel, ridge),
-        out_shape=[jax.ShapeDtypeStruct(image.shape, f32)] * 3,
-        in_specs=[smem, smem] + whole(len(grams) + 5) + in_hbm(4),
+        out_shape=[jax.ShapeDtypeStruct(image.shape, f32)] * 2 + [jax.ShapeDtypeStruct(packed, f32)],
+        in_specs=[smem, smem] + whole(len(grams) + 6),
         out_specs=in_hbm(3),
         scratch_shapes=[
-            pltpu.VMEM(before.shape, f32),
-            pltpu.VMEM(after.shape, f32),
-            pltpu.VMEM(image.shape, f32),
-            pltpu.VMEM(flat, f32),
             pltpu.VMEM(image.shape, f32),
             pltpu.VMEM(image.shape, f32),
-            pltpu.VMEM(image.shape, f32),
+            pltpu.VMEM(packed, f32),
+            pltpu.VMEM((2, channels, side), f32),
             pltpu.VMEM(flat, bf16),
             pltpu.VMEM(flat, bf16),
-            pltpu.VMEM((2, channels, side), f32),
-            pltpu.SemaphoreType.DMA((4,)),
+            pltpu.VMEM((flat[0] // HALVES, side), f32),
             pltpu.SemaphoreType.DMA((3, PARTS)),
         ],
         compiler_params=pltpu.CompilerParams(vmem_limit_bytes=24 * MIB),
         name="dual",
-    )(bound, edges, *grams, bound[:, None], image, image.reshape(flat), up, down, before, after, dual, low.reshape(flat))
+    )(bound, even, *grams, image, image.reshape(flat), first, second, dual, low.reshape(flat))
 
 
 def per_device(
@@ -593,7 +604,6 @@
     channels, rows_here, _ = lowrank_dual.shape
     devices = lax.axis_size(RING)
     pieces = lax.axis_size("pix")
-    here = lax.axis_index(RING)
     flat = (channels * rows_here, side)
 
     facet_image = lax.all_to_all(
@@ -606,28 +616,27 @@
     table = jnp.asarray(table)
     entries, bands_of = plan_blocks(tile_index[0], block_count[0], bands, chunks)
     y, hist = forward(image[0], visibilities[:, 0], cells[0], block_count, table, sizes)
-    edge_rows = jnp.stack([wavelet_dual[:, 0], wavelet_dual[:, -1]])
-    edges = jnp.stack([here > 0, here < devices - 1]).astype(f32)
-    facet_image, y, entries, bands_of, edge_rows, edges = lax.optimization_barrier(
-        (facet_image, y, entries, bands_of, edge_rows, edges)
+    even = (1 - lax.axis_index(RING) % 2).astype(jnp.int32)[None]
+    facet_image, y, entries, bands_of, even = lax.optimization_barrier(
+        (facet_image, y, entries, bands_of, even)
     )
 
-    up, down = halo_rows(facet_image.reshape(flat), edge_rows)
-    ahead = [(i, i + 1) for i in range(devices - 1)]
-    before = lax.ppermute(up, RING, ahead)
-    after = lax.ppermute(down, RING, [(j, i) for i, j in ahead])
-    gram = local_gram(lowrank_dual.reshape(flat), facet_image.reshape(flat), channels)
-    grams = [gram] + [
-        lax.ppermute(gram, "pix", [(i, (i + s) % pieces) for i in range(pieces)]) for s in range(1, pieces)
-    ]
+    first, second = local_gram(even, lowrank_dual.reshape(flat), facet_image.reshape(flat), channels)
+    first_got = lax.ppermute(first, RING, [(i, i ^ 1) for i in range(devices)])
+    inner = [(i, i + 1) for i in range(1, devices - 1, 2)]
+    second_got = lax.ppermute(second, RING, inner + [(j, i) for i, j in inner])
+    grams = [first[:, side : side + channels], first_got[:, side : side + channels]]
+    for turn in range(1, pieces.bit_length() - 1):
+        gram = sum(grams)
+        grams = [gram, lax.ppermute(gram, "pix", [(i, i ^ (1 << turn)) for i in range(pieces)])]
     ridge = float(rows_here * side * pieces)
-    wavelet_next, lowrank_next, direction = dual_update(
-        ridge, wavelet_bound, edges, grams, facet_image, up, down, before, after, wavelet_dual, lowrank_dual
+    wavelet_next, lowrank_next, packed = dual_update(
+        ridge, wavelet_bound, even, grams, facet_image, first_got, second_got, wavelet_dual, lowrank_dual
     )
-    direction, y = lax.optimization_barrier((direction, y))
-    returned = lax.all_to_all(direction, RING, split_axis=0, concat_axis=0, tiled=True)
+    packed, y = lax.optimization_barrier((packed, y))
+    returned = lax.all_to_all(packed, RING, split_axis=0, concat_axis=0, tiled=True)
     base = adjoint(entries, bands_of, image[0], y, hist, table, sizes)
-    image_next = final_image(base, returned.reshape(side, side))
+    image_next = final_image(base, returned)
     return (image_next[None], lowrank_next, wavelet_next)
 
 

time: 92.5 us -> 86.2 us (0.932)
  waiting for transfers between devices: 22.8 us -> 30.1 us
  Pallas kernels: 40.9 us -> 34.1 us
  starting transfers between devices: 19.8 us -> 15.6 us
  local copies, waits for them, and re-layouts: 3.02 us -> 0.6 us
    all_to_all x1, waiting for transfers between devices: 8.02 us -> 14.3 us  [per_device(): lax.all_to_all(packed, RING, split_axis=0, concat_axis=0, tiled=True)]
    ppermute x5 -> x3, starting transfers between devices: 8.86 us -> 4.67 us  [the longest x1 4.17 us: per_device(): second_got = lax.ppermute(second, RING, inner + [(j, i) for i, j in inner])]
    pallas_call x1, Pallas kernels: 18.5 us -> 14.9 us  [adjoint(): pl.pallas_call(functools.partial(adjoint_kernel, sizes), out_shape=jax.Sh...]
    unnamed x10 -> x6, local copies, waits for them, and re-layouts: 2.23 us -> 0.01 us
    pallas_call x1, Pallas kernels: 7.63 us -> 5.78 us  [dual_update(): pl.pallas_call(functools.partial(dual_kernel, ridge), out_shape=[jax.Shap...]
    all_to_all x1, waiting for transfers between devices: 9.7 us -> 11.4 us  [per_device(): lax.all_to_all(image.reshape(devices, rows_here, side), RING, split_axis=...]
    pallas_call x1, Pallas kernels: 11.1 us -> 9.64 us  [forward(): pl.pallas_call(functools.partial(forward_kernel, sizes[:4]), out_shape=[j...]
    pallas_call x2 -> x1, Pallas kernels: 2.43 us -> 1.69 us  [local_gram(): pl.pallas_call(gram_kernel, out_shape=[jax.ShapeDtypeStruct((channels, n)...]
  transfers between devices with their start and end apart: 7 -> 5, of which waited for: 4 -> 4; matrix products, arithmetic and copies ran while one was open for 5% -> 5% of each run, Pallas kernels for 34% -> 29%
where the time goes in v2:
time: 86.2 us; the launch traced here: 85.9 us
  Pallas kernels  34.1 us (40%)
  waiting for transfers between devices  30.1 us (35%)
  starting transfers between devices  15.6 us (18%)
  other arithmetic  4.05 us (5%)
  between operations  1.42 us (2%)
    pallas_call x1, Pallas kernels, adjoint(): pl.pallas_call(functools.partial(adjoint_kernel, sizes), out_shape=jax.Sh...  14.9 us
    all_to_all x1, waiting for transfers between devices, per_device(): lax.all_to_all(packed, RING, split_axis=0, concat_axis=0, tiled=True)  14.3 us
    all_to_all x1, waiting for transfers between devices, per_device(): lax.all_to_all(image.reshape(devices, rows_here, side), RING, split_axis=...  11.4 us
    pallas_call x1, Pallas kernels, forward(): pl.pallas_call(functools.partial(forward_kernel, sizes[:4]), out_shape=[j...  9.64 us
    all_to_all x1, starting transfers between devices, per_device(): lax.all_to_all(image.reshape(devices, rows_here, side), RING, split_axis=...  7.1 us
    pallas_call x1, Pallas kernels, dual_update(): pl.pallas_call(functools.partial(dual_kernel, ridge), out_shape=[jax.Shap...  5.78 us
    ppermute x1, starting transfers between devices, per_device(): second_got = lax.ppermute(second, RING, inner + [(j, i) for i, j in inner])  4.17 us
    all_to_all x1, starting transfers between devices, per_device(): lax.all_to_all(packed, RING, split_axis=0, concat_axis=0, tiled=True)  3.83 us
  transfers between devices with their start and end apart: 5, of which 4 were waited for; matrix products, arithmetic and copies ran while one was open for 5% of the time, Pallas kernels for 29%

profile of v2, /device:TPU:1, one launch (start us, length us, event | category | flops | bytes accessed | tf_op | source)
XLA Modules:
  0.0 85.9 jit_solution(2123284594893857789)
XLA Ops:
  0.6 0.0 copy-start
  0.6 0.0 copy-start.1
  0.7 0.0 copy-start.2
  0.7 7.1 %all-to-all-start = ((f32[32,16,512]{2,1,0:T(8,128)}), f32[32,16,512]{2,1,0:T(8,128)S(1)}, u32[]{:S(2)}, u32[]{:S(2)}) async-start(f32[32,16,512]{2,1,0:T(8,128)} %bitcast.20), calls=%async_computation | async-start | bytes 2097152 | tf_op jit(solution)/shard_map/all_to_all | solution.py:609
  8.4 0.7 compare_select_fusion.1
  9.1 0.1 convert_reduce_fusion.1
  9.3 0.1 select_reduce_fusion.2
  9.4 0.6 slice.9
  10.0 0.7 compare_select_fusion.7
  10.7 0.1 select_reduce_fusion.1
  10.8 0.2 convert_reduce_fusion
  10.9 9.6 %forward.1 = (bf16[2,8,512,256]{3,2,1,0:T(8,128)(2,1)}, f32[257,24,128]{2,1,0:T(8,128)}) custom-call(s32[1]{0:T(128)} %copy.14.live, f32[512,512]{1,0:T(8,128)} %bitcast.21, s32[256,128]{1,0:T(8,128)} %bitcast.25, f32[2,256,128]{2,1,0:T(8,128)} %bitcast.24, f32[1472,128]{1,0:T(8,128)} %constant.84.clone.table_in), custom_call_target="tpu_custom_call" | custom-call | tf_op jit(solution)/shard_map/forward/pallas_call | solution.py:295
  20.6 0.1 convert_reduce_fusion.2
  20.7 1.3 %pad_add_fusion.bands_of = s32[26]{0:T(128)} fusion(s32[1]{0:T(128)} %slice.9, s32[25]{0:T(128)S(1)} %broadcast_minimum_fusion), kind=kLoop, calls=%fused_computation.32 | loop fusion | flops 26 | bytes 208 | tf_op jit(solution)/shard_map/concatenate | solution.py:101
  22.0 0.2 select_reduce_fusion
  22.1 0.6 broadcast_add_fusion.entries
  22.7 11.4 %all-to-all-done.refs_2_ = f32[32,16,512]{2,1,0:T(8,128)S(1)} async-done(((f32[32,16,512]{2,1,0:T(8,128)}), f32[32,16,512]{2,1,0:T(8,128)S(1)}, u32[]{:S(2)}, u32[]{:S(2)}) %all-to-all-start) | async-done | bytes 1048608 | tf_op jit(solution)/shard_map/all_to_all | solution.py:609
  34.1 0.0 copy-done
  34.1 1.7 %gram.1 = (f32[32,640]{1,0:T(8,128)S(1)}, f32[32,512]{1,0:T(8,128)S(1)}) custom-call(s32[1]{0:T(128)} %bitcast.10.even, f32[512,512]{1,0:T(8,128)S(1)} %bitcast.18, f32[512,512]{1,0:T(8,128)S(1)} %bitcast.16), custom_call_target="tpu_custom_call" | custom-call | tf_op jit(solution)/shard_map/gram/pallas_call | solution.py:499
  35.8 0.1 collective-permute-start
  35.9 4.2 %collective-permute-start.2 = (f32[32,512]{1,0:T(8,128)S(1)}, f32[32,512]{1,0:T(8,128)S(1)}, u32[]{:S(2)}, u32[]{:S(2)}) collective-permute-start(f32[32,512]{1,0:T(8,128)S(1)} %get-tuple-element.23), channel_id=1, source_target_pairs={{1,2},{3,4},{5,6},{7,8},{9,10},{11,12},{13,14},{15,16},{17,18},{19... | collective-permute-start | bytes 196616 | tf_op jit(solution)/shard_map/ppermute | solution.py:627
  40.1 0.0 collective-permute-done.refs_4_
  40.1 0.4 collective-permute-start.1
  40.5 3.2 %collective-permute-done.2.refs_5_ = f32[32,512]{1,0:T(8,128)S(1)} collective-permute-done((f32[32,512]{1,0:T(8,128)S(1)}, f32[32,512]{1,0:T(8,128)S(1)}, u32[]{:S(2)}, u32[]{:S(2)}) %collective-permute-start.2) | collective-permute-done | bytes 65568 | tf_op jit(solution)/shard_map/ppermute | solution.py:627
  43.8 1.2 %collective-permute-done.1.refs_1_ = f32[32,32]{1,0:T(8,128)S(1)} collective-permute-done((f32[32,32]{1,0:T(8,128)S(1)}, f32[32,32]{1,0:T(8,128)S(1)}, u32[]{:S(2)}, u32[]{:S(2)}) %collective-permute-start.1) | collective-permute-done | bytes 4128 | tf_op jit(solution)/shard_map/ppermute | solution.py:631
  44.9 0.0 copy-done.1
  44.9 0.0 copy-done.2
  45.0 5.8 %dual.1 = (f32[32,16,512]{2,1,0:T(8,128)}, f32[32,16,512]{2,1,0:T(8,128)}, f32[32,8,1152]{2,1,0:T(8,128)}) custom-call(f32[32]{0:T(128)S(1)} %copy-done.2, s32[1]{0:T(128)} %bitcast.10.even, f32[32,32]{1,0:T(8,128)S(1)} %slice_add_fusion.refs_0_, f32[32,32]{1,0:T(8,128)S(1)} %collective-permute-done.1.refs_1_, f32[32,16,512]{2,1,0:T(8,128)S(1)} %all-to-all-done.refs_2_, ...), custom_call_target="tpu_custom_call" | custom-call | tf_op jit(solution)/shard_map/dual/pallas_call | solution.py:580
  50.7 3.8 %all-to-all-start.1 = ((f32[32,8,1152]{2,1,0:T(8,128)}), f32[32,8,1152]{2,1,0:T(8,128)S(1)}, u32[]{:S(2)}, u32[]{:S(2)}) async-start(f32[32,8,1152]{2,1,0:T(8,128)} %get-tuple-element.28), calls=%async_computation.1 | async-start | bytes 2359296 | tf_op jit(solution)/shard_map/all_to_all | solution.py:637
  54.6 14.9 %adjoint.1.base_in = f32[512,512]{1,0:T(8,128)} custom-call(s32[400]{0:T(512)} %broadcast_add_fusion.entries, s32[26]{0:T(128)} %pad_add_fusion.bands_of, f32[512,512]{1,0:T(8,128)} %bitcast.22, bf16[2,8,512,256]{3,2,1,0:T(8,128)(2,1)} %get-tuple-element.26.y_in, f32[257,24,128]{2,1,0:T(8,128)} %get-tuple-element.27.hist_in, f32[1472,128]{1,0:T(8,128)} %constant.84.clone.table_in), custom_call_target="tpu_custom_call" | custom-call | tf_op jit(solution)/shard_map/adjoint/pallas_call | solution.py:327
  69.4 14.3 %all-to-all-done.1.sent_in = f32[32,8,1152]{2,1,0:T(8,128)S(1)} async-done(((f32[32,8,1152]{2,1,0:T(8,128)}), f32[32,8,1152]{2,1,0:T(8,128)S(1)}, u32[]{:S(2)}, u32[]{:S(2)}) %all-to-all-start.1) | async-done | bytes 1179680 | tf_op jit(solution)/shard_map/all_to_all | solution.py:637
  83.7 2.2 %final.1 = f32[512,512]{1,0:T(8,128)} custom-call(f32[512,512]{1,0:T(8,128)} %adjoint.1.base_in, f32[32,8,1152]{2,1,0:T(8,128)S(1)} %all-to-all-done.1.sent_in), custom_call_target="tpu_custom_call", output_to_operand_aliasing={{}: (0, {})} | custom-call | tf_op jit(solution)/shard_map/final/pallas_call | solution.py:557
  (6 shorter events, 0.0 us)
Async XLA Ops:
  0.6 33.5 %copy-start = (f32[32,16,512]{2,1,0:T(8,128)S(1)}, f32[32,16,512]{2,1,0:T(8,128)}, u32[]{:S(2)}) copy-start(f32[32,16,512]{2,1,0:T(8,128)} %param.14) | copy-start | bytes 3145732
  0.6 44.3 %copy-start.1 = (f32[32,16,512]{2,1,0:T(8,128)S(1)}, f32[32,16,512]{2,1,0:T(8,128)}, u32[]{:S(2)}) copy-start(f32[32,16,512]{2,1,0:T(8,128)} %refs_6_.1) | copy-start | bytes 3145732
  0.7 44.3 %copy-start.2 = (f32[32]{0:T(128)S(1)}, f32[32]{0:T(128)}, u32[]{:S(2)}) copy-start(f32[32]{0:T(128)} %bound.1) | copy-start | bytes 388
  0.7 33.5 %all-to-all-start = ((f32[32,16,512]{2,1,0:T(8,128)}), f32[32,16,512]{2,1,0:T(8,128)S(1)}, u32[]{:S(2)}, u32[]{:S(2)}) async-start(f32[32,16,512]{2,1,0:T(8,128)} %bitcast.20), calls=%async_computation | async-start | bytes 2097152 | tf_op jit(solution)/shard_map/all_to_all | solution.py:609
  35.8 4.3 %collective-permute-start = (f32[32,640]{1,0:T(8,128)S(1)}, f32[32,640]{1,0:T(8,128)S(1)}, u32[]{:S(2)}, u32[]{:S(2)}) collective-permute-start(f32[32,640]{1,0:T(8,128)S(1)} %get-tuple-element.22), channel_id=1, source_target_pairs={{0,1},{1,0},{2,3},{3,2},{4,5},{5,4},{6,7},{7,6},{8,9},{9,8},{10,11... | collective-permute-start | bytes 245768 | tf_op jit(solution)/shard_map/ppermute | solution.py:625
  35.9 7.8 %collective-permute-start.2 = (f32[32,512]{1,0:T(8,128)S(1)}, f32[32,512]{1,0:T(8,128)S(1)}, u32[]{:S(2)}, u32[]{:S(2)}) collective-permute-start(f32[32,512]{1,0:T(8,128)S(1)} %get-tuple-element.23), channel_id=1, source_target_pairs={{1,2},{3,4},{5,6},{7,8},{9,10},{11,12},{13,14},{15,16},{17,18},{19... | collective-permute-start | bytes 196616 | tf_op jit(solution)/shard_map/ppermute | solution.py:627
  40.1 4.8 %collective-permute-start.1 = (f32[32,32]{1,0:T(8,128)S(1)}, f32[32,32]{1,0:T(8,128)S(1)}, u32[]{:S(2)}, u32[]{:S(2)}) collective-permute-start(f32[32,32]{1,0:T(8,128)S(1)} %slice_add_fusion.refs_0_), channel_id=1, source_target_pairs={{0,2},{1,3},{2,0},{3,1},{4,6},{5,7},{6,4},{7,5},{8,10},{9,11},{10,... | collective-permute-start | bytes 12296 | tf_op jit(solution)/shard_map/ppermute | solution.py:631
  50.7 33.0 %all-to-all-start.1 = ((f32[32,8,1152]{2,1,0:T(8,128)}), f32[32,8,1152]{2,1,0:T(8,128)S(1)}, u32[]{:S(2)}, u32[]{:S(2)}) async-start(f32[32,8,1152]{2,1,0:T(8,128)} %get-tuple-element.28), calls=%async_computation.1 | async-start | bytes 2359296 | tf_op jit(solution)/shard_map/all_to_all | solution.py:637

commit v3 on v2

--- a/solution.py
+++ b/solution.py
@@ -15,6 +15,7 @@
 GROUP = 16
 PARTS = 4
 HALVES = 1
+PIECES = 4
 RING = ("facet", "pix")
 
 highest = lax.Precision.HIGHEST
@@ -351,28 +352,31 @@
     )(entries, bands_of, plane, y, hist, table)
 
 
-def gram_kernel(even, dual, image, first, second):
-    channels, side = second.shape
+def edge_kernel(even, image, second):
+    channels = second.shape[0]
     rows = image.shape[0] // channels
-    left, right = jnp.where(even[0] == 1, rows - 1, 0), jnp.where(even[0] == 1, 0, rows - 1)
+    at = jnp.where(even[0] == 1, 0, rows - 1)
     for c in range(channels):
-        first[c : c + 1, :side] = image[pl.ds(c * rows + left, 1), :]
-        second[c : c + 1] = image[pl.ds(c * rows + right, 1), :]
+        second[c : c + 1] = image[pl.ds(c * rows + at, 1), :]
+
+
+def gram_kernel(even, dual, image, first):
+    channels = first.shape[0]
+    side = image.shape[1]
+    rows = image.shape[0] // channels
+    at = jnp.where(even[0] == 1, rows - 1, 0)
+    for c in range(channels):
+        first[c : c + 1, :side] = image[pl.ds(c * rows + at, 1), :]
     first[:, side:] = jnp.zeros((channels, first.shape[1] - side), f32)
     pick, match = row_maps(dual.shape[0], channels)
     high, low = split(dual[...] + sigma_step * image[...])
-    full = jnp.where(match, nt(high, high) + nt(high, low) + nt(low, high), 0.0)
-
-    def three(x):
-        a, rest = split(x)
-        b, c = split(x - a.astype(f32))
-        return a, b, c
-
+    full = jnp.where(match, nt(high, high) + nt(high, 2.0 * low), 0.0)
     half = sum(
         lax.dot_general(pick, part, (((0,), (0,)), ((), ())), preferred_element_type=f32)
-        for part in three(full)
+        for part in split(full)
     )
-    first[:, side : side + channels] = sum(jnp.dot(part, pick, preferred_element_type=f32) for part in three(half))
+    gram = sum(jnp.dot(part, pick, preferred_element_type=f32) for part in split(half))
+    first[:, side : side + channels] = 0.5 * (gram + gram.T)
 
 
 def packing(rows, side):
@@ -414,6 +418,8 @@
                 packed[c, k : k + 1, wide:] = -0.5 * slope[:1, lanes]
                 packed[c, short // 2 + k : short // 2 + k + 1, wide:] = -0.5 * slope[rows - 1 :, lanes]
 
+    pick, match = row_maps(total, channels)
+    b_hi[...], b_lo[...] = split(low[...] + sigma_step * flat_image[...])
     gram = grams[0][...]
     for other in grams[1:]:
         gram = gram + other[...]
@@ -436,8 +442,6 @@
     for part in range(PARTS):
         copy(1, part).start()
     root_hi, root_lo = split(inverse * (math.sqrt(ridge) * lax.rsqrt(trace)))
-    b_hi[...], b_lo[...] = split(low[...] + sigma_step * flat_image[...])
-    pick, match = row_maps(total, channels)
     half = total // HALVES
 
     for h in range(HALVES):
@@ -493,52 +497,52 @@
     return pick, i == j
 
 
+def edge_rows(even, image, channels):
+    return pl.pallas_call(
+        edge_kernel,
+        out_shape=jax.ShapeDtypeStruct((channels, image.shape[1]), f32),
+        in_specs=[pl.BlockSpec(memory_space=pltpu.SMEM)] + whole(1),
+        out_specs=whole(1)[0],
+        compiler_params=pltpu.CompilerParams(vmem_limit_bytes=8 * MIB),
+        name="edge",
+    )(even, image)
+
+
 def local_gram(even, dual, image, channels):
-    side = image.shape[1]
-    lanes = side + -(-channels // 128) * 128
+    lanes = image.shape[1] + -(-channels // 128) * 128
     return pl.pallas_call(
         gram_kernel,
-        out_shape=[jax.ShapeDtypeStruct((channels, n), f32) for n in (lanes, side)],
+        out_shape=jax.ShapeDtypeStruct((channels, lanes), f32),
         in_specs=[pl.BlockSpec(memory_space=pltpu.SMEM)] + whole(2),
-        out_specs=whole(2),
+        out_specs=whole(1)[0],
         compiler_params=pltpu.CompilerParams(vmem_limit_bytes=12 * MIB),
         name="gram",
     )(even, dual, image)
 
 
-def final_kernel(base_in, sent_in, out_ref, base, sent, out, base_sem, sent_sem, out_sem):
-    devices, short, lanes = sent.shape
+def final_kernel(base_in, sent, out_ref, base, base_sem, out_sem):
+    devices, short, _ = sent.shape
     side = base.shape[1]
     rows = base.shape[0] // devices
     _, wide, spare = packing(rows, side)
-    step = devices // PARTS
-
-    def reads(part):
-        at, to = pl.ds(part * step * rows, step * rows), pl.ds(part * step, step)
-        return (
-            pltpu.make_async_copy(base_in.at[at], base.at[at], base_sem.at[part]),
-            pltpu.make_async_copy(sent_in.at[to], sent.at[to], sent_sem.at[part]),
-        )
+    step = devices // PIECES
+
+    def read(part):
+        at = pl.ds(part * step * rows, step * rows)
+        return pltpu.make_async_copy(base_in.at[at], base.at[at], base_sem.at[part])
 
     def write(part):
         at = pl.ds(part * step * rows, step * rows)
-        return pltpu.make_async_copy(out.at[at], out_ref.at[at], out_sem.at[part])
+        return pltpu.make_async_copy(base.at[at], out_ref.at[at], out_sem.at[part])
 
     def beside(d, first):
         return jnp.concatenate([sent[d, first + k : first + k + 1, wide:] for k in range(short // 2)], axis=1)
 
-    def wait(part):
-        for read in reads(part):
-            read.wait()
-
-    for part in range(PARTS):
-        for read in reads(part):
-            read.start()
-    wait(0)
+    for part in range(PIECES):
+        read(part).start()
     row = lax.broadcasted_iota(jnp.int32, (short, side), 0)
-    for part in range(PARTS):
-        if part + 1 < PARTS:
-            wait(part + 1)
+    for part in range(PIECES):
+        read(part).wait()
         for d in range(part * step, (part + 1) * step):
             for h in range(rows // short):
                 at = slice(d * rows + h * short, d * rows + (h + 1) * short)
@@ -547,9 +551,9 @@
                     left = jnp.where(row == 0, left - beside(d - 1, short // 2), left)
                 if (h + 1) * short == rows and d + 1 < devices:
                     left = jnp.where(row == short - 1, left - beside(d + 1, 0), left)
-                out[at] = jnp.maximum(left, 0.0)
+                base[at] = jnp.maximum(left, 0.0)
         write(part).start()
-    for part in range(PARTS):
+    for part in range(PIECES):
         write(part).wait()
 
 
@@ -557,14 +561,9 @@
     return pl.pallas_call(
         final_kernel,
         out_shape=jax.ShapeDtypeStruct(base.shape, f32),
-        in_specs=in_hbm(2),
+        in_specs=in_hbm(1) + whole(1),
         out_specs=in_hbm(1)[0],
-        scratch_shapes=[
-            pltpu.VMEM(base.shape, f32),
-            pltpu.VMEM(sent.shape, f32),
-            pltpu.VMEM(base.shape, f32),
-        ]
-        + [pltpu.SemaphoreType.DMA((PARTS,))] * 3,
+        scratch_shapes=[pltpu.VMEM(base.shape, f32)] + [pltpu.SemaphoreType.DMA((PIECES,))] * 2,
         input_output_aliases={0: 0},
         compiler_params=pltpu.CompilerParams(vmem_limit_bytes=8 * MIB),
         name="final",
@@ -621,10 +620,11 @@
         (facet_image, y, entries, bands_of, even)
     )
 
-    first, second = local_gram(even, lowrank_dual.reshape(flat), facet_image.reshape(flat), channels)
+    inner = [(i, i + 1) for i in range(1, devices - 1, 2)]
+    second = edge_rows(even, facet_image.reshape(flat), channels)
+    second_got = lax.ppermute(second, RING, inner + [(j, i) for i, j in inner])
+    first = local_gram(even, lowrank_dual.reshape(flat), facet_image.reshape(flat), channels)
     first_got = lax.ppermute(first, RING, [(i, i ^ 1) for i in range(devices)])
-    inner = [(i, i + 1) for i in range(1, devices - 1, 2)]
-    second_got = lax.ppermute(second, RING, inner + [(j, i) for i, j in inner])
     grams = [first[:, side : side + channels], first_got[:, side : side + channels]]
     for turn in range(1, pieces.bit_length() - 1):
         gram = sum(grams)

time: 86.2 us -> 85.7 us (level)
  waiting for transfers between devices: 30.1 us -> 24.9 us
  Pallas kernels: 34.1 us -> 38.7 us
    all_to_all x1, waiting for transfers between devices: 14.3 us -> 10.7 us  [per_device(): lax.all_to_all(packed, RING, split_axis=0, concat_axis=0, tiled=True)]
    pallas_call x1, Pallas kernels: 14.9 us -> 18.5 us  [adjoint(): pl.pallas_call(functools.partial(adjoint_kernel, sizes), out_shape=jax.Sh...]
    all_to_all x1, waiting for transfers between devices: 11.4 us -> 9.83 us  [per_device(): lax.all_to_all(image.reshape(devices, rows_here, side), RING, split_axis=...]
    pallas_call x1, Pallas kernels: 9.64 us -> 11.1 us  [forward(): pl.pallas_call(functools.partial(forward_kernel, sizes[:4]), out_shape=[j...]
  transfers between devices with their start and end apart: 5 -> 5, of which waited for: 4 -> 4; matrix products, arithmetic and copies ran while one was open for 5% -> 5% of each run, Pallas kernels for 29% -> 35%
where the time goes in v3:
time: 85.7 us; the launch traced here: 85.3 us
  Pallas kernels  38.7 us (45%)
  waiting for transfers between devices  24.9 us (29%)
  starting transfers between devices  15.5 us (18%)
  other arithmetic  4.05 us (5%)
  between operations  1.5 us (2%)
    pallas_call x1, Pallas kernels, adjoint(): pl.pallas_call(functools.partial(adjoint_kernel, sizes), out_shape=jax.Sh...  18.5 us
    pallas_call x1, Pallas kernels, forward(): pl.pallas_call(functools.partial(forward_kernel, sizes[:4]), out_shape=[j...  11.1 us
    all_to_all x1, waiting for transfers between devices, per_device(): lax.all_to_all(packed, RING, split_axis=0, concat_axis=0, tiled=True)  10.7 us
    all_to_all x1, waiting for transfers between devices, per_device(): lax.all_to_all(image.reshape(devices, rows_here, side), RING, split_axis=...  9.83 us
    all_to_all x1, starting transfers between devices, per_device(): lax.all_to_all(image.reshape(devices, rows_here, side), RING, split_axis=...  7.1 us
    pallas_call x1, Pallas kernels, dual_update(): pl.pallas_call(functools.partial(dual_kernel, ridge), out_shape=[jax.Shap...  5.75 us
    ppermute x1, starting transfers between devices, per_device(): second_got = lax.ppermute(second, RING, inner + [(j, i) for i, j in inner])  4.16 us
    all_to_all x1, starting transfers between devices, per_device(): lax.all_to_all(packed, RING, split_axis=0, concat_axis=0, tiled=True)  3.82 us
  transfers between devices with their start and end apart: 5, of which 4 were waited for; matrix products, arithmetic and copies ran while one was open for 5% of the time, Pallas kernels for 35%

profile of v3, /device:TPU:1, one launch (start us, length us, event | category | flops | bytes accessed | tf_op | source)
XLA Modules:
  0.0 85.3 jit_solution(17751613177989105143)
XLA Ops:
  0.6 0.0 copy-start
  0.6 7.1 %all-to-all-start = ((f32[32,16,512]{2,1,0:T(8,128)}), f32[32,16,512]{2,1,0:T(8,128)S(1)}, u32[]{:S(2)}, u32[]{:S(2)}) async-start(f32[32,16,512]{2,1,0:T(8,128)} %bitcast.21), calls=%async_computation | async-start | bytes 2097152 | tf_op jit(solution)/shard_map/all_to_all | solution.py:608
  7.7 0.0 copy-start.1
  7.8 0.0 copy-start.2
  8.5 0.7 compare_select_fusion.1
  9.2 0.1 convert_reduce_fusion.1
  9.3 0.1 select_reduce_fusion.2
  9.5 0.6 slice.9
  10.1 0.7 compare_select_fusion.7
  10.8 0.1 select_reduce_fusion.1
  10.8 0.2 convert_reduce_fusion
  11.0 11.1 %forward.1 = (bf16[2,8,512,256]{3,2,1,0:T(8,128)(2,1)}, f32[257,24,128]{2,1,0:T(8,128)}) custom-call(s32[1]{0:T(128)} %copy.14.live, f32[512,512]{1,0:T(8,128)} %bitcast.22, s32[256,128]{1,0:T(8,128)} %bitcast.26, f32[2,256,128]{2,1,0:T(8,128)} %bitcast.25, f32[1472,128]{1,0:T(8,128)} %constant.84.clone.table_in), custom_call_target="tpu_custom_call" | custom-call | tf_op jit(solution)/shard_map/forward/pallas_call | solution.py:296
  22.1 0.1 convert_reduce_fusion.2
  22.2 1.3 %pad_add_fusion.bands_of = s32[26]{0:T(128)} fusion(s32[1]{0:T(128)} %slice.9, s32[25]{0:T(128)S(1)} %broadcast_minimum_fusion), kind=kLoop, calls=%fused_computation.32 | loop fusion | flops 26 | bytes 208 | tf_op jit(solution)/shard_map/concatenate | solution.py:102
  23.5 0.2 select_reduce_fusion
  23.7 0.6 broadcast_add_fusion.entries
  24.3 9.8 %all-to-all-done.refs_2_ = f32[32,16,512]{2,1,0:T(8,128)S(1)} async-done(((f32[32,16,512]{2,1,0:T(8,128)}), f32[32,16,512]{2,1,0:T(8,128)S(1)}, u32[]{:S(2)}, u32[]{:S(2)}) %all-to-all-start) | async-done | bytes 1048608 | tf_op jit(solution)/shard_map/all_to_all | solution.py:608
  34.1 0.0 copy-done
  34.1 1.3 %gram.1 = f32[32,640]{1,0:T(8,128)S(1)} custom-call(s32[1]{0:T(128)} %bitcast.10.even, f32[512,512]{1,0:T(8,128)S(1)} %bitcast.19, f32[512,512]{1,0:T(8,128)S(1)} %bitcast.16), custom_call_target="tpu_custom_call" | custom-call | tf_op jit(solution)/shard_map/gram/pallas_call | solution.py:513
  35.4 0.0 collective-permute-start
  35.4 0.1 edge.1
  35.5 4.2 %collective-permute-start.2 = (f32[32,512]{1,0:T(8,128)S(1)}, f32[32,512]{1,0:T(8,128)S(1)}, u32[]{:S(2)}, u32[]{:S(2)}) collective-permute-start(f32[32,512]{1,0:T(8,128)S(1)} %edge.1), channel_id=1, source_target_pairs={{1,2},{3,4},{5,6},{7,8},{9,10},{11,12},{13,14},{15,16},{17,18},{19... | collective-permute-start | bytes 196616 | tf_op jit(solution)/shard_map/ppermute | solution.py:625
  39.7 0.0 collective-permute-done.refs_4_
  39.7 0.4 collective-permute-start.1
  40.1 3.2 %collective-permute-done.2.refs_5_ = f32[32,512]{1,0:T(8,128)S(1)} collective-permute-done((f32[32,512]{1,0:T(8,128)S(1)}, f32[32,512]{1,0:T(8,128)S(1)}, u32[]{:S(2)}, u32[]{:S(2)}) %collective-permute-start.2) | collective-permute-done | bytes 65568 | tf_op jit(solution)/shard_map/ppermute | solution.py:625
  43.4 1.2 %collective-permute-done.1.refs_1_ = f32[32,32]{1,0:T(8,128)S(1)} collective-permute-done((f32[32,32]{1,0:T(8,128)S(1)}, f32[32,32]{1,0:T(8,128)S(1)}, u32[]{:S(2)}, u32[]{:S(2)}) %collective-permute-start.1) | collective-permute-done | bytes 4128 | tf_op jit(solution)/shard_map/ppermute | solution.py:631
  44.6 0.0 copy-done.1
  44.6 0.0 copy-done.2
  44.6 5.8 %dual.1 = (f32[32,16,512]{2,1,0:T(8,128)}, f32[32,16,512]{2,1,0:T(8,128)}, f32[32,8,1152]{2,1,0:T(8,128)}) custom-call(f32[32]{0:T(128)S(1)} %copy-done.2, s32[1]{0:T(128)} %bitcast.10.even, f32[32,32]{1,0:T(8,128)S(1)} %slice_add_fusion.refs_0_, f32[32,32]{1,0:T(8,128)S(1)} %collective-permute-done.1.refs_1_, f32[32,16,512]{2,1,0:T(8,128)S(1)} %all-to-all-done.refs_2_, ...), custom_call_target="tpu_custom_call" | custom-call | tf_op jit(solution)/shard_map/dual/pallas_call | solution.py:579
  50.3 3.8 %all-to-all-start.1 = ((f32[32,8,1152]{2,1,0:T(8,128)}), f32[32,8,1152]{2,1,0:T(8,128)S(1)}, u32[]{:S(2)}, u32[]{:S(2)}) async-start(f32[32,8,1152]{2,1,0:T(8,128)} %get-tuple-element.24), calls=%async_computation.1 | async-start | bytes 2359296 | tf_op jit(solution)/shard_map/all_to_all | solution.py:637
  54.2 18.5 %adjoint.1.base_in = f32[512,512]{1,0:T(8,128)} custom-call(s32[400]{0:T(512)} %broadcast_add_fusion.entries, s32[26]{0:T(128)} %pad_add_fusion.bands_of, f32[512,512]{1,0:T(8,128)} %bitcast.23, bf16[2,8,512,256]{3,2,1,0:T(8,128)(2,1)} %get-tuple-element.22.y_in, f32[257,24,128]{2,1,0:T(8,128)} %get-tuple-element.23.hist_in, f32[1472,128]{1,0:T(8,128)} %constant.84.clone.table_in), custom_call_target="tpu_custom_call" | custom-call | tf_op jit(solution)/shard_map/adjoint/pallas_call | solution.py:328
  72.6 10.7 %all-to-all-done.1.sent = f32[32,8,1152]{2,1,0:T(8,128)S(1)} async-done(((f32[32,8,1152]{2,1,0:T(8,128)}), f32[32,8,1152]{2,1,0:T(8,128)S(1)}, u32[]{:S(2)}, u32[]{:S(2)}) %all-to-all-start.1) | async-done | bytes 1179680 | tf_op jit(solution)/shard_map/all_to_all | solution.py:637
  83.3 2.0 %final.1 = f32[512,512]{1,0:T(8,128)} custom-call(f32[512,512]{1,0:T(8,128)} %adjoint.1.base_in, f32[32,8,1152]{2,1,0:T(8,128)S(1)} %all-to-all-done.1.sent), custom_call_target="tpu_custom_call", output_to_operand_aliasing={{}: (0, {})} | custom-call | tf_op jit(solution)/shard_map/final/pallas_call | solution.py:561
  (6 shorter events, 0.0 us)
Async XLA Ops:
  0.6 33.5 %copy-start = (f32[32,16,512]{2,1,0:T(8,128)S(1)}, f32[32,16,512]{2,1,0:T(8,128)}, u32[]{:S(2)}) copy-start(f32[32,16,512]{2,1,0:T(8,128)} %param.14) | copy-start | bytes 3145732
  0.6 33.5 %all-to-all-start = ((f32[32,16,512]{2,1,0:T(8,128)}), f32[32,16,512]{2,1,0:T(8,128)S(1)}, u32[]{:S(2)}, u32[]{:S(2)}) async-start(f32[32,16,512]{2,1,0:T(8,128)} %bitcast.21), calls=%async_computation | async-start | bytes 2097152 | tf_op jit(solution)/shard_map/all_to_all | solution.py:608
  7.7 36.8 %copy-start.1 = (f32[32,16,512]{2,1,0:T(8,128)S(1)}, f32[32,16,512]{2,1,0:T(8,128)}, u32[]{:S(2)}) copy-start(f32[32,16,512]{2,1,0:T(8,128)} %refs_6_.1) | copy-start | bytes 3145732
  7.8 36.8 %copy-start.2 = (f32[32]{0:T(128)S(1)}, f32[32]{0:T(128)}, u32[]{:S(2)}) copy-start(f32[32]{0:T(128)} %bound.1) | copy-start | bytes 388
  35.4 4.3 %collective-permute-start = (f32[32,640]{1,0:T(8,128)S(1)}, f32[32,640]{1,0:T(8,128)S(1)}, u32[]{:S(2)}, u32[]{:S(2)}) collective-permute-start(f32[32,640]{1,0:T(8,128)S(1)} %gram.1), channel_id=1, source_target_pairs={{0,1},{1,0},{2,3},{3,2},{4,5},{5,4},{6,7},{7,6},{8,9},{9,8},{10,11... | collective-permute-start | bytes 245768 | tf_op jit(solution)/shard_map/ppermute | solution.py:627
  35.5 7.9 %collective-permute-start.2 = (f32[32,512]{1,0:T(8,128)S(1)}, f32[32,512]{1,0:T(8,128)S(1)}, u32[]{:S(2)}, u32[]{:S(2)}) collective-permute-start(f32[32,512]{1,0:T(8,128)S(1)} %edge.1), channel_id=1, source_target_pairs={{1,2},{3,4},{5,6},{7,8},{9,10},{11,12},{13,14},{15,16},{17,18},{19... | collective-permute-start | bytes 196616 | tf_op jit(solution)/shard_map/ppermute | solution.py:625
  39.7 4.8 %collective-permute-start.1 = (f32[32,32]{1,0:T(8,128)S(1)}, f32[32,32]{1,0:T(8,128)S(1)}, u32[]{:S(2)}, u32[]{:S(2)}) collective-permute-start(f32[32,32]{1,0:T(8,128)S(1)} %slice_add_fusion.refs_0_), channel_id=1, source_target_pairs={{0,2},{1,3},{2,0},{3,1},{4,6},{5,7},{6,4},{7,5},{8,10},{9,11},{10,... | collective-permute-start | bytes 12296 | tf_op jit(solution)/shard_map/ppermute | solution.py:631
  50.3 33.0 %all-to-all-start.1 = ((f32[32,8,1152]{2,1,0:T(8,128)}), f32[32,8,1152]{2,1,0:T(8,128)S(1)}, u32[]{:S(2)}, u32[]{:S(2)}) async-start(f32[32,8,1152]{2,1,0:T(8,128)} %get-tuple-element.24), calls=%async_computation.1 | async-start | bytes 2359296 | tf_op jit(solution)/shard_map/all_to_all | solution.py:637

commit v4 on v3

--- a/solution.py
+++ b/solution.py
@@ -352,21 +352,14 @@
     )(entries, bands_of, plane, y, hist, table)
 
 
-def edge_kernel(even, image, second):
-    channels = second.shape[0]
-    rows = image.shape[0] // channels
-    at = jnp.where(even[0] == 1, 0, rows - 1)
-    for c in range(channels):
-        second[c : c + 1] = image[pl.ds(c * rows + at, 1), :]
-
-
-def gram_kernel(even, dual, image, first):
+def gram_kernel(even, dual, image, first, second):
     channels = first.shape[0]
     side = image.shape[1]
     rows = image.shape[0] // channels
     at = jnp.where(even[0] == 1, rows - 1, 0)
     for c in range(channels):
         first[c : c + 1, :side] = image[pl.ds(c * rows + at, 1), :]
+        second[c : c + 1] = image[pl.ds(c * rows + rows - 1 - at, 1), :]
     first[:, side:] = jnp.zeros((channels, first.shape[1] - side), f32)
     pick, match = row_maps(dual.shape[0], channels)
     high, low = split(dual[...] + sigma_step * image[...])
@@ -497,24 +490,13 @@
     return pick, i == j
 
 
-def edge_rows(even, image, channels):
-    return pl.pallas_call(
-        edge_kernel,
-        out_shape=jax.ShapeDtypeStruct((channels, image.shape[1]), f32),
-        in_specs=[pl.BlockSpec(memory_space=pltpu.SMEM)] + whole(1),
-        out_specs=whole(1)[0],
-        compiler_params=pltpu.CompilerParams(vmem_limit_bytes=8 * MIB),
-        name="edge",
-    )(even, image)
-
-
 def local_gram(even, dual, image, channels):
     lanes = image.shape[1] + -(-channels // 128) * 128
     return pl.pallas_call(
         gram_kernel,
-        out_shape=jax.ShapeDtypeStruct((channels, lanes), f32),
+        out_shape=[jax.ShapeDtypeStruct((channels, n), f32) for n in (lanes, image.shape[1])],
         in_specs=[pl.BlockSpec(memory_space=pltpu.SMEM)] + whole(2),
-        out_specs=whole(1)[0],
+        out_specs=whole(2),
         compiler_params=pltpu.CompilerParams(vmem_limit_bytes=12 * MIB),
         name="gram",
     )(even, dual, image)
@@ -621,9 +603,8 @@
     )
 
     inner = [(i, i + 1) for i in range(1, devices - 1, 2)]
-    second = edge_rows(even, facet_image.reshape(flat), channels)
+    first, second = local_gram(even, lowrank_dual.reshape(flat), facet_image.reshape(flat), channels)
     second_got = lax.ppermute(second, RING, inner + [(j, i) for i, j in inner])
-    first = local_gram(even, lowrank_dual.reshape(flat), facet_image.reshape(flat), channels)
     first_got = lax.ppermute(first, RING, [(i, i ^ 1) for i in range(devices)])
     grams = [first[:, side : side + channels], first_got[:, side : side + channels]]
     for turn in range(1, pieces.bit_length() - 1):

time: 85.7 us -> 85.8 us (level)
  Pallas kernels: 38.7 us -> 40.9 us
  waiting for transfers between devices: 24.9 us -> 22.9 us
    pallas_call x1, Pallas kernels: 18.5 us -> 19.7 us  [adjoint(): pl.pallas_call(functools.partial(adjoint_kernel, sizes), out_shape=jax.Sh...]
    all_to_all x1, waiting for transfers between devices: 10.7 us -> 9.45 us  [per_device(): lax.all_to_all(packed, RING, split_axis=0, concat_axis=0, tiled=True)]
    pallas_call x1, Pallas kernels: 11.1 us -> 12.1 us  [forward(): pl.pallas_call(functools.partial(forward_kernel, sizes[:4]), out_shape=[j...]
  transfers between devices with their start and end apart: 5 -> 5, of which waited for: 4 -> 4; matrix products, arithmetic and copies ran while one was open for 5% -> 5% of each run, Pallas kernels for 35% -> 37%
where the time goes in v4:
time: 85.8 us; the launch traced here: 85.4 us
  Pallas kernels  40.9 us (48%)
  waiting for transfers between devices  22.9 us (27%)
  starting transfers between devices  15.6 us (18%)
  other arithmetic  4.05 us (5%)
  between operations  1.42 us (2%)
    pallas_call x1, Pallas kernels, adjoint(): pl.pallas_call(functools.partial(adjoint_kernel, sizes), out_shape=jax.Sh...  19.7 us
    pallas_call x1, Pallas kernels, forward(): pl.pallas_call(functools.partial(forward_kernel, sizes[:4]), out_shape=[j...  12.1 us
    all_to_all x1, waiting for transfers between devices, per_device(): lax.all_to_all(packed, RING, split_axis=0, concat_axis=0, tiled=True)  9.45 us
    all_to_all x1, waiting for transfers between devices, per_device(): lax.all_to_all(image.reshape(devices, rows_here, side), RING, split_axis=...  8.98 us
    all_to_all x1, starting transfers between devices, per_device(): lax.all_to_all(image.reshape(devices, rows_here, side), RING, split_axis=...  7.1 us
    pallas_call x1, Pallas kernels, dual_update(): pl.pallas_call(functools.partial(dual_kernel, ridge), out_shape=[jax.Shap...  5.79 us
    ppermute x1, starting transfers between devices, per_device(): second_got = lax.ppermute(second, RING, inner + [(j, i) for i, j in inner])  4.16 us
    all_to_all x1, starting transfers between devices, per_device(): lax.all_to_all(packed, RING, split_axis=0, concat_axis=0, tiled=True)  3.81 us
  transfers between devices with their start and end apart: 5, of which 4 were waited for; matrix products, arithmetic and copies ran while one was open for 5% of the time, Pallas kernels for 37%

profile of v4, /device:TPU:1, one launch (start us, length us, event | category | flops | bytes accessed | tf_op | source)
XLA Modules:
  0.0 85.4 jit_solution(4818295513829694872)
XLA Ops:
  0.6 0.0 copy-start
  0.6 0.0 copy-start.1
  0.7 0.0 copy-start.2
  0.7 7.1 %all-to-all-start = ((f32[32,16,512]{2,1,0:T(8,128)}), f32[32,16,512]{2,1,0:T(8,128)S(1)}, u32[]{:S(2)}, u32[]{:S(2)}) async-start(f32[32,16,512]{2,1,0:T(8,128)} %bitcast.20), calls=%async_computation | async-start | bytes 2097152 | tf_op jit(solution)/shard_map/all_to_all | solution.py:590
  8.4 0.7 compare_select_fusion.1
  9.1 0.1 convert_reduce_fusion.1
  9.3 0.1 select_reduce_fusion.2
  9.4 0.6 slice.9
  10.0 0.7 compare_select_fusion.7
  10.7 0.1 select_reduce_fusion.1
  10.8 0.2 convert_reduce_fusion
  10.9 12.1 %forward.1 = (bf16[2,8,512,256]{3,2,1,0:T(8,128)(2,1)}, f32[257,24,128]{2,1,0:T(8,128)}) custom-call(s32[1]{0:T(128)} %copy.14.live, f32[512,512]{1,0:T(8,128)} %bitcast.21, s32[256,128]{1,0:T(8,128)} %bitcast.25, f32[2,256,128]{2,1,0:T(8,128)} %bitcast.24, f32[1472,128]{1,0:T(8,128)} %constant.84.clone.table_in), custom_call_target="tpu_custom_call" | custom-call | tf_op jit(solution)/shard_map/forward/pallas_call | solution.py:296
  23.0 0.1 convert_reduce_fusion.2
  23.1 1.3 %pad_add_fusion.bands_of = s32[26]{0:T(128)} fusion(s32[1]{0:T(128)} %slice.9, s32[25]{0:T(128)S(1)} %broadcast_minimum_fusion), kind=kLoop, calls=%fused_computation.32 | loop fusion | flops 26 | bytes 208 | tf_op jit(solution)/shard_map/concatenate | solution.py:102
  24.4 0.2 select_reduce_fusion
  24.6 0.6 broadcast_add_fusion.entries
  25.1 9.0 %all-to-all-done.refs_2_ = f32[32,16,512]{2,1,0:T(8,128)S(1)} async-done(((f32[32,16,512]{2,1,0:T(8,128)}), f32[32,16,512]{2,1,0:T(8,128)S(1)}, u32[]{:S(2)}, u32[]{:S(2)}) %all-to-all-start) | async-done | bytes 1048608 | tf_op jit(solution)/shard_map/all_to_all | solution.py:590
  34.1 0.0 copy-done
  34.1 1.4 %gram.1 = (f32[32,640]{1,0:T(8,128)S(1)}, f32[32,512]{1,0:T(8,128)S(1)}) custom-call(s32[1]{0:T(128)} %bitcast.10.even, f32[512,512]{1,0:T(8,128)S(1)} %bitcast.18, f32[512,512]{1,0:T(8,128)S(1)} %bitcast.16), custom_call_target="tpu_custom_call" | custom-call | tf_op jit(solution)/shard_map/gram/pallas_call | solution.py:495
  35.5 0.1 collective-permute-start
  35.6 4.2 %collective-permute-start.2 = (f32[32,512]{1,0:T(8,128)S(1)}, f32[32,512]{1,0:T(8,128)S(1)}, u32[]{:S(2)}, u32[]{:S(2)}) collective-permute-start(f32[32,512]{1,0:T(8,128)S(1)} %get-tuple-element.23), channel_id=1, source_target_pairs={{1,2},{3,4},{5,6},{7,8},{9,10},{11,12},{13,14},{15,16},{17,18},{19... | collective-permute-start | bytes 196616 | tf_op jit(solution)/shard_map/ppermute | solution.py:607
  39.8 0.0 collective-permute-done.refs_4_
  39.8 0.4 collective-permute-start.1
  40.2 3.2 %collective-permute-done.2.refs_5_ = f32[32,512]{1,0:T(8,128)S(1)} collective-permute-done((f32[32,512]{1,0:T(8,128)S(1)}, f32[32,512]{1,0:T(8,128)S(1)}, u32[]{:S(2)}, u32[]{:S(2)}) %collective-permute-start.2) | collective-permute-done | bytes 65568 | tf_op jit(solution)/shard_map/ppermute | solution.py:607
  43.4 1.2 %collective-permute-done.1.refs_1_ = f32[32,32]{1,0:T(8,128)S(1)} collective-permute-done((f32[32,32]{1,0:T(8,128)S(1)}, f32[32,32]{1,0:T(8,128)S(1)}, u32[]{:S(2)}, u32[]{:S(2)}) %collective-permute-start.1) | collective-permute-done | bytes 4128 | tf_op jit(solution)/shard_map/ppermute | solution.py:612
  44.6 0.0 copy-done.1
  44.6 0.0 copy-done.2
  44.6 5.8 %dual.1 = (f32[32,16,512]{2,1,0:T(8,128)}, f32[32,16,512]{2,1,0:T(8,128)}, f32[32,8,1152]{2,1,0:T(8,128)}) custom-call(f32[32]{0:T(128)S(1)} %copy-done.2, s32[1]{0:T(128)} %bitcast.10.even, f32[32,32]{1,0:T(8,128)S(1)} %slice_add_fusion.refs_0_, f32[32,32]{1,0:T(8,128)S(1)} %collective-permute-done.1.refs_1_, f32[32,16,512]{2,1,0:T(8,128)S(1)} %all-to-all-done.refs_2_, ...), custom_call_target="tpu_custom_call" | custom-call | tf_op jit(solution)/shard_map/dual/pallas_call | solution.py:561
  50.4 3.8 %all-to-all-start.1 = ((f32[32,8,1152]{2,1,0:T(8,128)}), f32[32,8,1152]{2,1,0:T(8,128)S(1)}, u32[]{:S(2)}, u32[]{:S(2)}) async-start(f32[32,8,1152]{2,1,0:T(8,128)} %get-tuple-element.28), calls=%async_computation.1 | async-start | bytes 2359296 | tf_op jit(solution)/shard_map/all_to_all | solution.py:618
  54.3 19.7 %adjoint.1.base_in = f32[512,512]{1,0:T(8,128)} custom-call(s32[400]{0:T(512)} %broadcast_add_fusion.entries, s32[26]{0:T(128)} %pad_add_fusion.bands_of, f32[512,512]{1,0:T(8,128)} %bitcast.22, bf16[2,8,512,256]{3,2,1,0:T(8,128)(2,1)} %get-tuple-element.26.y_in, f32[257,24,128]{2,1,0:T(8,128)} %get-tuple-element.27.hist_in, f32[1472,128]{1,0:T(8,128)} %constant.84.clone.table_in), custom_call_target="tpu_custom_call" | custom-call | tf_op jit(solution)/shard_map/adjoint/pallas_call | solution.py:328
  73.9 9.4 %all-to-all-done.1.sent = f32[32,8,1152]{2,1,0:T(8,128)S(1)} async-done(((f32[32,8,1152]{2,1,0:T(8,128)}), f32[32,8,1152]{2,1,0:T(8,128)S(1)}, u32[]{:S(2)}, u32[]{:S(2)}) %all-to-all-start.1) | async-done | bytes 1179680 | tf_op jit(solution)/shard_map/all_to_all | solution.py:618
  83.4 2.0 %final.1 = f32[512,512]{1,0:T(8,128)} custom-call(f32[512,512]{1,0:T(8,128)} %adjoint.1.base_in, f32[32,8,1152]{2,1,0:T(8,128)S(1)} %all-to-all-done.1.sent), custom_call_target="tpu_custom_call", output_to_operand_aliasing={{}: (0, {})} | custom-call | tf_op jit(solution)/shard_map/final/pallas_call | solution.py:543
  (6 shorter events, 0.0 us)
Async XLA Ops:
  0.6 33.5 %copy-start = (f32[32,16,512]{2,1,0:T(8,128)S(1)}, f32[32,16,512]{2,1,0:T(8,128)}, u32[]{:S(2)}) copy-start(f32[32,16,512]{2,1,0:T(8,128)} %param.14) | copy-start | bytes 3145732
  0.6 44.0 %copy-start.1 = (f32[32,16,512]{2,1,0:T(8,128)S(1)}, f32[32,16,512]{2,1,0:T(8,128)}, u32[]{:S(2)}) copy-start(f32[32,16,512]{2,1,0:T(8,128)} %refs_6_.1) | copy-start | bytes 3145732
  0.7 44.0 %copy-start.2 = (f32[32]{0:T(128)S(1)}, f32[32]{0:T(128)}, u32[]{:S(2)}) copy-start(f32[32]{0:T(128)} %bound.1) | copy-start | bytes 388
  0.7 33.5 %all-to-all-start = ((f32[32,16,512]{2,1,0:T(8,128)}), f32[32,16,512]{2,1,0:T(8,128)S(1)}, u32[]{:S(2)}, u32[]{:S(2)}) async-start(f32[32,16,512]{2,1,0:T(8,128)} %bitcast.20), calls=%async_computation | async-start | bytes 2097152 | tf_op jit(solution)/shard_map/all_to_all | solution.py:590
  35.5 4.3 %collective-permute-start = (f32[32,640]{1,0:T(8,128)S(1)}, f32[32,640]{1,0:T(8,128)S(1)}, u32[]{:S(2)}, u32[]{:S(2)}) collective-permute-start(f32[32,640]{1,0:T(8,128)S(1)} %get-tuple-element.22), channel_id=1, source_target_pairs={{0,1},{1,0},{2,3},{3,2},{4,5},{5,4},{6,7},{7,6},{8,9},{9,8},{10,11... | collective-permute-start | bytes 245768 | tf_op jit(solution)/shard_map/ppermute | solution.py:608
  35.6 7.9 %collective-permute-start.2 = (f32[32,512]{1,0:T(8,128)S(1)}, f32[32,512]{1,0:T(8,128)S(1)}, u32[]{:S(2)}, u32[]{:S(2)}) collective-permute-start(f32[32,512]{1,0:T(8,128)S(1)} %get-tuple-element.23), channel_id=1, source_target_pairs={{1,2},{3,4},{5,6},{7,8},{9,10},{11,12},{13,14},{15,16},{17,18},{19... | collective-permute-start | bytes 196616 | tf_op jit(solution)/shard_map/ppermute | solution.py:607
  39.8 4.8 %collective-permute-start.1 = (f32[32,32]{1,0:T(8,128)S(1)}, f32[32,32]{1,0:T(8,128)S(1)}, u32[]{:S(2)}, u32[]{:S(2)}) collective-permute-start(f32[32,32]{1,0:T(8,128)S(1)} %slice_add_fusion.refs_0_), channel_id=1, source_target_pairs={{0,2},{1,3},{2,0},{3,1},{4,6},{5,7},{6,4},{7,5},{8,10},{9,11},{10,... | collective-permute-start | bytes 12296 | tf_op jit(solution)/shard_map/ppermute | solution.py:612
  50.4 32.9 %all-to-all-start.1 = ((f32[32,8,1152]{2,1,0:T(8,128)}), f32[32,8,1152]{2,1,0:T(8,128)S(1)}, u32[]{:S(2)}, u32[]{:S(2)}) async-start(f32[32,8,1152]{2,1,0:T(8,128)} %get-tuple-element.28), calls=%async_computation.1 | async-start | bytes 2359296 | tf_op jit(solution)/shard_map/all_to_all | solution.py:618
